TPU v7x, 32 devices: a whole 2x2x4 slice. The times are simulated.
32 devices in a mesh: chan: 8 (over z, x), section: 4 (over y, core).
Axes of the slice: x: 2, y: 2, z: 4, core: 2. Of those that a mesh axis runs over, the one named last changes fastest.
Arguments:
- voltages: bfloat16 [2, 2, 36, 16, 188, 128], P(None, None, 'section', 'chan'), may hold values from -32 to 32
- weights: bfloat16 [2, 36, 16, 36, 188], P(None, 'section', 'chan'), may hold values from -4 to 4
- sat_index: int32 [2, 8, 2], P(None, 'chan'), may hold values from 0 to 63, as said below
- offsets: int32 [2, 128], replicated, may hold values from 0 to 127
- angles: float32 [64, 188], replicated, may hold values from -3 to 3
Outputs:
- visibilities: float32 [2, 36, 16, 1296], P(None, 'section', 'chan')
- new_weights: bfloat16 [2, 36, 16, 36, 188], P(None, 'section', 'chan')
Inputs may be any that keep to these rules, and one draw needn't show every extreme that they name: `sat_index`: catalogue rows of the satellites nulled in each cycle and block of 2 channels.
All inputs are finite; a program needn't handle non-finite values.
Results may differ from a plain program's by a relative error of at most 0.0065.
Values may be sent and summed in bfloat16 or wider, within the bound.
No kernel may reach another device: no remote copies, remote signals or barrier semaphores. Data moves between devices by JAX's collectives and lax.ppermute only.
A program may use at most 128 MiB of HBM per device.

v0:
```python
import functools

import jax
import jax.numpy as jnp
from jax import lax
from jax.experimental import pallas as pl
from jax.experimental.pallas import tpu as pltpu
from jax.sharding import PartitionSpec as P

LOADING = 100.0
F32 = jnp.float32
BF16 = jnp.bfloat16
SUB = 8


def rounded_up(size):
    return -(-size // SUB) * SUB


def spread_matrix(ports, chans):
    port = lax.broadcasted_iota(jnp.int32, (ports, ports * chans), 0) * chans
    lane = lax.broadcasted_iota(jnp.int32, (ports, ports * chans), 1)
    return jnp.where((lane >= port) & (lane < port + chans), 1.0, 0.0).astype(BF16)


def own_channel(rows, rows_per_chan, ports, chans):
    row = lax.broadcasted_iota(jnp.int32, (rows, ports * chans), 0)
    lane = lax.broadcasted_iota(jnp.int32, (rows, ports * chans), 1)
    return lax.rem(lax.div(row, rows_per_chan), chans) == lax.rem(lane, chans)


def split(value):
    high = value.astype(BF16)
    low = (value - high.astype(F32)).astype(BF16)
    return high, low


def dot(left, right):
    return jnp.dot(left, right, preferred_element_type=F32)


def dot_t(left, right):
    return lax.dot_general(left, right, (((1,), (1,)), ((), ())), preferred_element_type=F32)


def beams_of(weight_rows, spread, keep, x_real, x_imag):
    wide = jnp.where(keep, dot(weight_rows, spread), 0.0)
    half = wide.shape[0] // 2
    real, imag = wide[:half], wide[half:]
    on_real = jnp.concatenate([real, -imag]).astype(BF16)
    on_imag = jnp.concatenate([imag, real]).astype(BF16)
    return dot(on_real, x_real) + dot(on_imag, x_imag)


def put_beams(beam_rows, stage, dish, dims):
    groups, chans, group_beams, dishes, pad_beams = dims
    block = 2 * dishes
    for part in range(2):
        for f in range(chans):
            for g in range(groups):
                source = (part * chans + f) * pad_beams + g * group_beams
                first = g * stage_rows(dims) + f * group_beams * block + part * dishes + dish
                stage[pl.ds(first, group_beams, stride=block), :] = beam_rows[
                    source : source + group_beams
                ]


def stage_rows(dims):
    groups, chans, group_beams, dishes, pad_beams = dims
    return rounded_up(chans * group_beams * 2 * dishes)


def flush_beams(stage, out, dims):
    groups = dims[0]
    rows = out.shape[1]
    for g in range(groups):
        first = g * stage_rows(dims)
        out[g] = stage[first : first + rows, :].astype(BF16)


def first_beams_kernel(dims, x_ref, w_ref, out_ref, stage):
    dishes = x_ref.shape[2]
    chans = dims[1]
    ports = w_ref.shape[-1]
    spread = spread_matrix(ports, chans)
    keep = own_channel(w_ref.shape[1], dims[4], ports, chans)
    for d in range(dishes):
        rows = beams_of(w_ref[d], spread, keep, x_ref[0, 0, d], x_ref[0, 1, d])
        put_beams(rows, stage, d, dims)
    flush_beams(stage, out_ref, dims)


def nulls_kernel(sat_ref, sat_dn_ref, sat_up_ref, off_ref, ang_ref, x_ref,
                 own_ref, dn_ref, up_ref, phase, folded):
    cycles, _, dishes, wide, samples = x_ref.shape
    ports = ang_ref.shape[-1]
    chans = wide // ports
    slots = sat_ref.shape[-1]
    per_chan = 2 * slots
    rows = chans * per_chan
    spread = spread_matrix(ports, chans)
    lane_t = lax.broadcasted_iota(jnp.int32, (1, samples), 1)
    for c in range(cycles):
        for f in range(chans):
            beside = sat_dn_ref if f == 0 else sat_up_ref
            for s in range(slots):
                base = f * per_chan + s
                phase[pl.ds(c * rows + base, 1), :] = ang_ref[pl.ds(sat_ref[c, s], 1), :]
                phase[pl.ds(c * rows + base + slots, 1), :] = ang_ref[
                    pl.ds(beside[c, s], 1), :
                ]
    angle = phase[...]
    cosine, sine = jnp.cos(angle), jnp.sin(angle)
    keep4 = own_channel(4 * rows, per_chan, ports, chans)
    keep2 = own_channel(2 * rows, per_chan, ports, chans)
    for c in range(cycles):
        def count(j, total):
            return total + jnp.where(lane_t == off_ref[c, j], 1.0, 0.0)

        counts = lax.fori_loop(0, off_ref.shape[1], count, jnp.zeros((1, samples), F32), unroll=8)
        a_real = cosine[c * rows : (c + 1) * rows]
        a_imag = sine[c * rows : (c + 1) * rows]
        real_h, real_l = split(a_real)
        imag_h, imag_l = split(a_imag)
        column = jnp.concatenate(
            [real_h.astype(F32), real_l.astype(F32), imag_h.astype(F32), imag_l.astype(F32)]
        ).astype(BF16)
        wide_rows = jnp.where(keep4, dot(column, spread), 0.0)
        half = 2 * rows
        on_real = wide_rows.astype(BF16)
        on_imag = jnp.concatenate([wide_rows[half:], -wide_rows[:half]]).astype(BF16)
        for d in range(dishes):
            x_real, x_imag = x_ref[c, 0, d], x_ref[c, 1, d]
            inner = dot(on_real, x_real) + dot(on_imag, x_imag)
            inner_real = (inner[0:rows] + inner[rows:half]) * counts
            inner_imag = (inner[half : half + rows] + inner[half + rows :]) * counts
            real_h, real_l = split(inner_real)
            imag_h, imag_l = split(inner_imag)
            pieces = jnp.concatenate(
                [real_h.astype(F32), real_l.astype(F32), imag_h.astype(F32), imag_l.astype(F32)]
            )
            turned = jnp.concatenate([-pieces[half:], pieces[:half]])
            outer = dot_t(pieces.astype(BF16), x_real) + dot_t(turned.astype(BF16), x_imag)
            both = jnp.concatenate(
                [outer[0:rows] + outer[rows:half], outer[half : half + rows] + outer[half + rows :]]
            )
            first = (c * dishes + d) * 2 * rows
            folded[first : first + 2 * rows, :] = jnp.where(keep2, both, 0.0)
    high, low = split(folded[...])
    summed = dot_t(high, spread) + dot_t(low, spread)
    for c in range(cycles):
        for d in range(dishes):
            first = (c * dishes + d) * 2 * rows
            for part in range(2):
                block = summed[first + part * rows : first + (part + 1) * rows]
                own = block[0:slots]
                for f in range(1, chans):
                    own = own + block[f * per_chan : f * per_chan + slots]
                along = (cosine if part == 0 else sine)[c * rows : c * rows + slots]
                last = (chans - 1) * per_chan + slots
                where = slice(part * slots, (part + 1) * slots)
                own_ref[c, d, where, :] = own + LOADING * along
                dn_ref[c, d, where, :] = block[slots : 2 * slots]
                up_ref[c, d, where, :] = block[last : last + slots]


def null_rows(rows, own, beside, chans, pad_beams):
    slots = own.shape[0] // 2
    half = rows.shape[0] // 2
    reals, imags = [], []
    for f in range(chans):
        real = rows[f * pad_beams : (f + 1) * pad_beams]
        imag = rows[half + f * pad_beams : half + (f + 1) * pad_beams]
        null = own + beside[f]
        for s in range(slots):
            u_real = null[s : s + 1]
            u_imag = null[slots + s : slots + s + 1]
            inverse = 1.0 / jnp.sum(u_real * u_real + u_imag * u_imag, axis=-1, keepdims=True)
            c_real = jnp.sum(real * u_real + imag * u_imag, axis=-1, keepdims=True) * inverse
            c_imag = jnp.sum(imag * u_real - real * u_imag, axis=-1, keepdims=True) * inverse
            real = real - (u_real * c_real - u_imag * c_imag)
            imag = imag - (u_real * c_imag + u_imag * c_real)
        reals.append(real)
        imags.append(imag)
    return jnp.concatenate(reals + imags)


def next_beams_kernel(dims, x_ref, w_ref, own_ref, dn_ref, up_ref, out_ref, next_ref, stage):
    dishes = x_ref.shape[2]
    chans, pad_beams = dims[1], dims[4]
    ports = w_ref.shape[-1]
    spread = spread_matrix(ports, chans)
    keep = own_channel(w_ref.shape[1], pad_beams, ports, chans)
    for d in range(dishes):
        rows = null_rows(
            w_ref[d].astype(F32), own_ref[0, d], (dn_ref[0, d], up_ref[0, d]), chans, pad_beams
        ).astype(BF16)
        next_ref[d] = rows
        put_beams(
            beams_of(rows, spread, keep, x_ref[0, 0, d], x_ref[0, 1, d]), stage, d, dims
        )
    flush_beams(stage, out_ref, dims)


def last_nulls_kernel(dims, w_ref, own_ref, dn_ref, up_ref, next_ref):
    chans, pad_beams = dims[1], dims[4]
    for d in range(w_ref.shape[0]):
        next_ref[d] = null_rows(
            w_ref[d].astype(F32), own_ref[0, d], (dn_ref[0, d], up_ref[0, d]), chans, pad_beams
        ).astype(BF16)


def correlate_kernel(dims, scale, *refs):
    groups, chans, group_beams, dishes, _ = dims
    beam_refs, out_ref, gathered, sums = refs[:-3], refs[-3], refs[-2], refs[-1]
    all_dishes = groups * dishes
    pad_dishes = rounded_up(all_dishes)
    pairs = group_beams * chans
    pad_pairs = rounded_up(pairs)
    samples = gathered.shape[-1]
    block = 2 * dishes
    filler = jnp.zeros((pad_dishes, samples), F32)
    for i in range(len(beam_refs) * pairs * 2):
        gathered[i] = filler
    for i, beam_ref in enumerate(beam_refs):
        for g in range(groups):
            values = beam_ref[g].astype(F32)
            for f in range(chans):
                for b in range(group_beams):
                    for part in range(2):
                        first = (f * group_beams + b) * block + part * dishes
                        gathered[
                            (i * pairs + b * chans + f) * 2 + part,
                            g * dishes : (g + 1) * dishes,
                            :,
                        ] = values[first : first + dishes]
    for pair in range(pairs):
        total = None
        for i in range(len(beam_refs)):
            real = gathered[(i * pairs + pair) * 2]
            imag = gathered[(i * pairs + pair) * 2 + 1]
            top = jnp.concatenate([real, imag], axis=1)
            left = jnp.concatenate([top, jnp.concatenate([imag, -real], axis=1)]).astype(BF16)
            right = jnp.concatenate(
                [top, jnp.zeros((samples - pad_dishes, 2 * samples), F32)]
            ).astype(BF16)
            term = dot_t(left, right)
            total = term if total is None else total + term
        sums[pl.ds(pair, 2 * pad_dishes, stride=pad_pairs), :] = total * scale
    for part in range(2):
        pieces = []
        for d in range(all_dishes):
            first = (part * pad_dishes + d) * pad_pairs
            pieces.append(sums[first : first + pad_pairs, 0:all_dishes])
        flat = jnp.concatenate(pieces, axis=1)
        out_ref[part] = flat[:pairs]


def vmem():
    return pl.BlockSpec(memory_space=pltpu.VMEM)


def smem():
    return pl.BlockSpec(memory_space=pltpu.SMEM)


def per_device(voltages, weights, sat_index, offsets, angles):
    cycles, _, dishes, chans, ports, samples = voltages.shape
    beams = weights.shape[3]
    slots = sat_index.shape[2]
    groups = lax.axis_size("section")
    peers = lax.axis_size("chan")
    group_beams = beams // groups
    pad_beams = rounded_up(beams)
    dims = (groups, chans, group_beams, dishes, pad_beams)
    wide = ports * chans
    x = voltages.transpose(0, 1, 2, 4, 3, 5).reshape(cycles, 2, dishes, wide, samples)
    w = jnp.pad(weights, ((0, 0), (0, 0), (0, 0), (0, pad_beams - beams), (0, 0)))
    w = w.transpose(1, 0, 2, 3, 4).reshape(dishes, 2 * chans * pad_beams, ports)

    up = [(i, i + 1) for i in range(peers - 1)]
    down = [(i + 1, i) for i in range(peers - 1)]
    sat_dn = lax.ppermute(sat_index, "chan", up)
    sat_up = lax.ppermute(sat_index, "chan", down)

    chunk = 2 * chans * group_beams * dishes
    sent = jax.ShapeDtypeStruct((groups, chunk, samples), BF16)
    stage = pltpu.VMEM((groups * stage_rows(dims), samples), F32)
    w_rows = w.shape[1]

    def x_of(cycle):
        return pl.BlockSpec((1, 2, dishes, wide, samples), lambda i: (cycle, 0, 0, 0, 0))

    def whole(*shape):
        return pl.BlockSpec(shape, lambda i: (0,) * len(shape))

    first = pl.pallas_call(
        functools.partial(first_beams_kernel, dims),
        grid=(1,),
        out_shape=sent,
        in_specs=[x_of(0), whole(*w.shape)],
        out_specs=whole(*sent.shape),
        scratch_shapes=[stage],
        name="first_beams",
    )(x, w)
    first_all = lax.all_to_all(first, "section", split_axis=0, concat_axis=0, tiled=True)

    rows = chans * 2 * slots
    vectors = jax.ShapeDtypeStruct((cycles, dishes, 2 * slots, ports), F32)
    own, to_dn, to_up = pl.pallas_call(
        nulls_kernel,
        out_shape=(vectors,) * 3,
        in_specs=[smem(), smem(), smem(), smem(), vmem(), vmem()],
        out_specs=(vmem(),) * 3,
        scratch_shapes=[
            pltpu.VMEM((cycles * rows, ports), F32),
            pltpu.VMEM((cycles * dishes * 2 * rows, wide), F32),
        ],
        name="nulls",
    )(sat_index[:, 0], sat_dn[:, 0], sat_up[:, 0], offsets, angles, x)
    from_up = lax.ppermute(to_dn, "chan", down)
    from_dn = lax.ppermute(to_up, "chan", up)

    def vec_of(cycle):
        return pl.BlockSpec((1, dishes, 2 * slots, ports), lambda i: (cycle, 0, 0, 0))

    second, w_next = pl.pallas_call(
        functools.partial(next_beams_kernel, dims),
        grid=(1,),
        out_shape=(sent, jax.ShapeDtypeStruct(w.shape, BF16)),
        in_specs=[x_of(1), whole(*w.shape), vec_of(0), vec_of(0), vec_of(0)],
        out_specs=(whole(*sent.shape), whole(*w.shape)),
        scratch_shapes=[stage],
        name="next_beams",
    )(x, w, own, from_dn, from_up)
    second_all = lax.all_to_all(second, "section", split_axis=0, concat_axis=0, tiled=True)

    w_last = pl.pallas_call(
        functools.partial(last_nulls_kernel, dims),
        grid=(1,),
        out_shape=jax.ShapeDtypeStruct(w.shape, BF16),
        in_specs=[whole(*w.shape), vec_of(1), vec_of(1), vec_of(1)],
        out_specs=whole(*w.shape),
        name="last_nulls",
    )(w_next, own, from_dn, from_up)
    new_weights = w_last.reshape(dishes, 2, chans, pad_beams, ports)[:, :, :, :beams]
    new_weights = new_weights.transpose(1, 0, 2, 3, 4)

    all_dishes = dishes * groups
    pairs = group_beams * chans
    pad_dishes = rounded_up(all_dishes)
    vis = pl.pallas_call(
        functools.partial(correlate_kernel, dims, 1.0 / (cycles * samples)),
        out_shape=jax.ShapeDtypeStruct((2, pairs, all_dishes * all_dishes), F32),
        in_specs=[vmem(), vmem()],
        out_specs=vmem(),
        scratch_shapes=[
            pltpu.VMEM((cycles * pairs * 2, pad_dishes, samples), F32),
            pltpu.VMEM((2 * pad_dishes * rounded_up(pairs), samples), F32),
        ],
        name="correlate",
    )(first_all, second_all)
    vis = vis.reshape(2, group_beams, chans, all_dishes * all_dishes)
    return vis, new_weights


def solution(mesh):
    placed = (
        P(None, None, "section", "chan", None, None),
        P(None, "section", "chan", None, None),
        P(None, "chan", None),
        P(),
        P(),
    )
    return jax.shard_map(
        per_device,
        mesh=mesh,
        in_specs=placed,
        out_specs=(P(None, "section", "chan", None), P(None, "section", "chan", None, None)),
        check_vma=False,
    )
```

profile of v0, /device:TPU:0, one launch (start us, length us, event | category | flops | bytes accessed | tf_op | source)
XLA Modules:
  0.0 61.2 jit_solution(1109735721616380452)
XLA Ops:
  0.6 1.8 %pad_bitcast_fusion = bf16[9,2,2,40,188]{4,2,3,0,1:T(2,128)(2,1)S(1)} fusion(bf16[2,9,2,36,188]{4,2,3,1,0:T(2,128)(2,1)} %param.6), kind=kLoop, calls=%fused_computation | loop fusion | bytes 1028736 | tf_op jit(solution)/shard_map/transpose | solution.py:279
  2.4 0.0 copy-start.4
  2.4 1.0 %copy.9 = bf16[9,2,2,40,188]{4,3,2,1,0:T(8,128)(2,1)} copy(bf16[9,2,2,40,188]{4,2,3,0,1:T(2,128)(2,1)S(1)} %pad_bitcast_fusion) | data formatting | bytes 1082880 | tf_op jit(solution)/shard_map/transpose | solution.py:279
  3.4 4.5 %first_beams.1 = bf16[4,324,128]{2,1,0:T(8,128)(2,1)} custom-call(bf16[2,2,9,376,128]{4,3,2,1,0:T(8,128)(2,1)} %bitcast.15, bf16[9,160,188]{2,1,0:T(8,128)(2,1)} %bitcast.18), custom_call_target="tpu_custom_call" | custom-call | tf_op jit(solution)/shard_map/first_beams/pallas_call | solution.py:297
  7.9 4.3 %all-to-all-start = ((bf16[4,324,128]{2,1,0:T(8,128)(2,1)}), bf16[4,324,128]{2,1,0:T(8,128)(2,1)S(1)}, u32[]{:S(2)}, u32[]{:S(2)}) async-start(bf16[4,324,128]{2,1,0:T(8,128)(2,1)} %first_beams.1), calls=%async_computation | async-start | bytes 671744 | tf_op jit(solution)/shard_map/all_to_all | solution.py:306
  12.2 0.0 copy-done.4
  12.2 1.3 %collective-permute-start.1 = (s32[2,1,2]{2,1,0:T(1,128)S(1)}, s32[2,1,2]{2,1,0:T(1,128)S(1)}, u32[]{:S(2)}, u32[]{:S(2)}) collective-permute-start(s32[2,1,2]{2,1,0:T(1,128)S(1)} %copy-done.4), channel_id=1, source_target_pairs={{4,0},{8,4},{12,8},{16,12},{20,16},{24,20},{28,24},{5,1},{9,5},{13... | collective-permute-start | bytes 56 | tf_op jit(solution)/shard_map/ppermute | solution.py:284
  13.5 4.7 %collective-permute-start = (s32[2,1,2]{2,1,0:T(1,128)S(1)}, s32[2,1,2]{2,1,0:T(1,128)S(1)}, u32[]{:S(2)}, u32[]{:S(2)}) collective-permute-start(s32[2,1,2]{2,1,0:T(1,128)S(1)} %copy-done.4), channel_id=1, source_target_pairs={{0,4},{4,8},{8,12},{12,16},{16,20},{20,24},{24,28},{1,5},{5,9},{9,... | collective-permute-start | bytes 56 | tf_op jit(solution)/shard_map/ppermute | solution.py:283
  18.2 0.0 collective-permute-done.1
  18.2 0.0 copy-start.5
  18.2 1.3 %collective-permute-done = s32[2,1,2]{2,1,0:T(1,128)S(1)} collective-permute-done((s32[2,1,2]{2,1,0:T(1,128)S(1)}, s32[2,1,2]{2,1,0:T(1,128)S(1)}, u32[]{:S(2)}, u32[]{:S(2)}) %collective-permute-start) | collective-permute-done | bytes 48 | tf_op jit(solution)/shard_map/ppermute | solution.py:283
  19.5 0.0 copy-start.6
  19.5 0.0 copy-done.5
  19.5 0.6 copy-done.6
  20.1 7.8 %nulls.1 = (f32[2,9,4,188]{3,2,1,0:T(4,128)}, f32[2,9,4,188]{3,2,1,0:T(4,128)}, f32[2,9,4,188]{3,2,1,0:T(4,128)}) custom-call(s32[2,2]{1,0:T(2,128)} %bitcast.23, s32[2,2]{1,0:T(2,128)} %bitcast.25, s32[2,2]{1,0:T(2,128)} %bitcast.24, s32[2,128]{1,0:T(2,128)} %off_ref.1, f32[64,188]{1,0:T(8,128)} %ang_ref.1, bf16[2,2,9,376,128]{4,3,2,1,0:T(8,128)(2,1)} %bitcast.16), custom_call_target="tpu_custom_call" | custom-call | tf_op jit(solution)/shard_map/nulls/pallas_call | solution.py:310
  27.8 4.8 %collective-permute-start.2 = (f32[2,9,4,188]{3,2,1,0:T(4,128)}, f32[2,9,4,188]{3,2,1,0:T(4,128)S(1)}, u32[]{:S(2)}, u32[]{:S(2)}) collective-permute-start(f32[2,9,4,188]{3,2,1,0:T(4,128)} %get-tuple-element.8), channel_id=1, source_target_pairs={{0,4},{4,8},{8,12},{12,16},{16,20},{20,24},{24,28},{1,5},{5,9},{9,... | collective-permute-start | bytes 162440 | tf_op jit(solution)/shard_map/ppermute | solution.py:322
  32.7 1.3 %collective-permute-start.3 = (f32[2,9,4,188]{3,2,1,0:T(4,128)}, f32[2,9,4,188]{3,2,1,0:T(4,128)S(1)}, u32[]{:S(2)}, u32[]{:S(2)}) collective-permute-start(f32[2,9,4,188]{3,2,1,0:T(4,128)} %get-tuple-element.9), channel_id=1, source_target_pairs={{4,0},{8,4},{12,8},{16,12},{20,16},{24,20},{28,24},{5,1},{9,5},{13... | collective-permute-start | bytes 162440 | tf_op jit(solution)/shard_map/ppermute | solution.py:321
  34.0 1.0 %collective-permute-done.2.dn_ref = f32[2,9,4,188]{3,2,1,0:T(4,128)S(1)} collective-permute-done((f32[2,9,4,188]{3,2,1,0:T(4,128)}, f32[2,9,4,188]{3,2,1,0:T(4,128)S(1)}, u32[]{:S(2)}, u32[]{:S(2)}) %collective-permute-start.2) | collective-permute-done | bytes 54176 | tf_op jit(solution)/shard_map/ppermute | solution.py:322
  34.9 5.3 %collective-permute-done.3.up_ref = f32[2,9,4,188]{3,2,1,0:T(4,128)S(1)} collective-permute-done((f32[2,9,4,188]{3,2,1,0:T(4,128)}, f32[2,9,4,188]{3,2,1,0:T(4,128)S(1)}, u32[]{:S(2)}, u32[]{:S(2)}) %collective-permute-start.3) | collective-permute-done | bytes 54176 | tf_op jit(solution)/shard_map/ppermute | solution.py:321
  40.3 0.0 copy-done.2
  40.3 0.6 %copy-done.3 = f32[2,9,4,188]{3,2,1,0:T(4,128)} copy-done((f32[2,9,4,188]{3,2,1,0:T(4,128)}, f32[2,9,4,188]{3,2,1,0:T(4,128)S(1)}, u32[]{:S(2)}) %copy-start.3) | copy-done | bytes 54168
  40.9 4.9 %next_beams.1 = (bf16[4,324,128]{2,1,0:T(8,128)(2,1)}, bf16[9,160,188]{2,1,0:T(8,128)(2,1)}) custom-call(bf16[2,2,9,376,128]{4,3,2,1,0:T(8,128)(2,1)} %bitcast.17, bf16[9,160,188]{2,1,0:T(8,128)(2,1)} %bitcast.19, f32[2,9,4,188]{3,2,1,0:T(4,128)} %get-tuple-element.7.own_ref, f32[2,9,4,188]{3,2,1,0:T(4,128)} %copy-done.2, f32[2,9,4,188]{3,2,1,0:T(4,128)} %copy-done.3), custom_call_target="tpu_custom_call" | custom-call | tf_op jit(solution)/shard_map/next_beams/pallas_call | solution.py:327
  45.8 0.0 all-to-all-done.refs_0_
  45.8 3.5 %all-to-all-start.1 = ((bf16[4,324,128]{2,1,0:T(8,128)(2,1)}), bf16[4,324,128]{2,1,0:T(8,128)(2,1)S(1)}, u32[]{:S(2)}, u32[]{:S(2)}) async-start(bf16[4,324,128]{2,1,0:T(8,128)(2,1)} %get-tuple-element.10), calls=%async_computation.1 | async-start | bytes 671744 | tf_op jit(solution)/shard_map/all_to_all | solution.py:336
  49.3 3.6 %last_nulls.1 = bf16[9,160,188]{2,1,0:T(8,128)(2,1)} custom-call(bf16[9,160,188]{2,1,0:T(8,128)(2,1)} %get-tuple-element.11.w_ref, f32[2,9,4,188]{3,2,1,0:T(4,128)} %get-tuple-element.7.own_ref, f32[2,9,4,188]{3,2,1,0:T(4,128)} %copy-done.2, f32[2,9,4,188]{3,2,1,0:T(4,128)} %copy-done.3), custom_call_target="tpu_custom_call" | custom-call | tf_op jit(solution)/shard_map/last_nulls/pallas_call | solution.py:338
  52.9 2.5 %copy.15 = bf16[9,2,2,36,188]{4,2,3,0,1:T(2,128)(2,1)} copy(bf16[9,2,2,36,188]{4,3,2,1,0:T(8,128)(2,1)} %bitcast.20) | data formatting | bytes 974592
  55.3 0.7 %all-to-all-done.1.refs_1_ = bf16[4,324,128]{2,1,0:T(8,128)(2,1)S(1)} async-done(((bf16[4,324,128]{2,1,0:T(8,128)(2,1)}), bf16[4,324,128]{2,1,0:T(8,128)(2,1)S(1)}, u32[]{:S(2)}, u32[]{:S(2)}) %all-to-all-start.1) | async-done | bytes 331808 | tf_op jit(solution)/shard_map/all_to_all | solution.py:336
  56.1 0.0 copy-done
  56.1 0.7 %copy-done.1 = bf16[4,324,128]{2,1,0:T(8,128)(2,1)} copy-done((bf16[4,324,128]{2,1,0:T(8,128)(2,1)}, bf16[4,324,128]{2,1,0:T(8,128)(2,1)S(1)}, u32[]{:S(2)}) %copy-start.1) | copy-done | bytes 331800
  56.8 2.6 %correlate.1 = f32[2,18,1296]{2,1,0:T(8,128)} custom-call(bf16[4,324,128]{2,1,0:T(8,128)(2,1)} %copy-done, bf16[4,324,128]{2,1,0:T(8,128)(2,1)} %copy-done.1), custom_call_target="tpu_custom_call" | custom-call | tf_op jit(solution)/shard_map/correlate/pallas_call | solution.py:352
  59.4 1.1 %copy.10 = f32[2,18,1296]{2,0,1:T(2,128)S(1)} copy(f32[2,18,1296]{2,1,0:T(8,128)} %correlate.1) | data formatting | bytes 373248 | tf_op jit(solution)/shard_map/correlate/pallas_call | solution.py:352
  60.4 0.8 %copy.12 = f32[2,9,2,1296]{3,2,1,0:T(2,128)} copy(f32[2,9,2,1296]{3,0,2,1:T(2,128)S(1)} %bitcast.21) | data formatting | bytes 373248
  (4 shorter events, 0.0 us)
Async XLA Ops:
  2.4 9.8 %copy-start.4 = (s32[2,1,2]{2,1,0:T(1,128)S(1)}, s32[2,1,2]{2,1,0:T(1,128)}, u32[]{:S(2)}) copy-start(s32[2,1,2]{2,1,0:T(1,128)} %param.7) | copy-start | bytes 52
  7.9 37.9 %all-to-all-start = ((bf16[4,324,128]{2,1,0:T(8,128)(2,1)}), bf16[4,324,128]{2,1,0:T(8,128)(2,1)S(1)}, u32[]{:S(2)}, u32[]{:S(2)}) async-start(bf16[4,324,128]{2,1,0:T(8,128)(2,1)} %first_beams.1), calls=%async_computation | async-start | bytes 671744 | tf_op jit(solution)/shard_map/all_to_all | solution.py:306
  12.2 6.0 %collective-permute-start.1 = (s32[2,1,2]{2,1,0:T(1,128)S(1)}, s32[2,1,2]{2,1,0:T(1,128)S(1)}, u32[]{:S(2)}, u32[]{:S(2)}) collective-permute-start(s32[2,1,2]{2,1,0:T(1,128)S(1)} %copy-done.4), channel_id=1, source_target_pairs={{4,0},{8,4},{12,8},{16,12},{20,16},{24,20},{28,24},{5,1},{9,5},{13... | collective-permute-start | bytes 56 | tf_op jit(solution)/shard_map/ppermute | solution.py:284
  13.5 6.0 %collective-permute-start = (s32[2,1,2]{2,1,0:T(1,128)S(1)}, s32[2,1,2]{2,1,0:T(1,128)S(1)}, u32[]{:S(2)}, u32[]{:S(2)}) collective-permute-start(s32[2,1,2]{2,1,0:T(1,128)S(1)} %copy-done.4), channel_id=1, source_target_pairs={{0,4},{4,8},{8,12},{12,16},{16,20},{20,24},{24,28},{1,5},{5,9},{9,... | collective-permute-start | bytes 56 | tf_op jit(solution)/shard_map/ppermute | solution.py:283
  18.2 1.3 %copy-start.5 = (s32[2,1,2]{2,1,0:T(1,128)}, s32[2,1,2]{2,1,0:T(1,128)S(1)}, u32[]{:S(2)}) copy-start(s32[2,1,2]{2,1,0:T(1,128)S(1)} %collective-permute-done.1) | copy-start | bytes 52
  19.5 0.6 copy-start.6
  27.8 7.1 %collective-permute-start.2 = (f32[2,9,4,188]{3,2,1,0:T(4,128)}, f32[2,9,4,188]{3,2,1,0:T(4,128)S(1)}, u32[]{:S(2)}, u32[]{:S(2)}) collective-permute-start(f32[2,9,4,188]{3,2,1,0:T(4,128)} %get-tuple-element.8), channel_id=1, source_target_pairs={{0,4},{4,8},{8,12},{12,16},{16,20},{20,24},{24,28},{1,5},{5,9},{9,... | collective-permute-start | bytes 162440 | tf_op jit(solution)/shard_map/ppermute | solution.py:322
  32.7 7.6 %collective-permute-start.3 = (f32[2,9,4,188]{3,2,1,0:T(4,128)}, f32[2,9,4,188]{3,2,1,0:T(4,128)S(1)}, u32[]{:S(2)}, u32[]{:S(2)}) collective-permute-start(f32[2,9,4,188]{3,2,1,0:T(4,128)} %get-tuple-element.9), channel_id=1, source_target_pairs={{4,0},{8,4},{12,8},{16,12},{20,16},{24,20},{28,24},{5,1},{9,5},{13... | collective-permute-start | bytes 162440 | tf_op jit(solution)/shard_map/ppermute | solution.py:321
  34.9 5.3 %copy-start.2 = (f32[2,9,4,188]{3,2,1,0:T(4,128)}, f32[2,9,4,188]{3,2,1,0:T(4,128)S(1)}, u32[]{:S(2)}) copy-start(f32[2,9,4,188]{3,2,1,0:T(4,128)S(1)} %collective-permute-done.2.dn_ref) | copy-start | bytes 162436
  40.3 0.6 %copy-start.3 = (f32[2,9,4,188]{3,2,1,0:T(4,128)}, f32[2,9,4,188]{3,2,1,0:T(4,128)S(1)}, u32[]{:S(2)}) copy-start(f32[2,9,4,188]{3,2,1,0:T(4,128)S(1)} %collective-permute-done.3.up_ref) | copy-start | bytes 162436
  45.8 10.2 %copy-start = (bf16[4,324,128]{2,1,0:T(8,128)(2,1)}, bf16[4,324,128]{2,1,0:T(8,128)(2,1)S(1)}, u32[]{:S(2)}) copy-start(bf16[4,324,128]{2,1,0:T(8,128)(2,1)S(1)} %all-to-all-done.refs_0_) | copy-start | bytes 995332
  45.8 10.2 %all-to-all-start.1 = ((bf16[4,324,128]{2,1,0:T(8,128)(2,1)}), bf16[4,324,128]{2,1,0:T(8,128)(2,1)S(1)}, u32[]{:S(2)}, u32[]{:S(2)}) async-start(bf16[4,324,128]{2,1,0:T(8,128)(2,1)} %get-tuple-element.10), calls=%async_computation.1 | async-start | bytes 671744 | tf_op jit(solution)/shard_map/all_to_all | solution.py:336
  56.1 0.7 %copy-start.1 = (bf16[4,324,128]{2,1,0:T(8,128)(2,1)}, bf16[4,324,128]{2,1,0:T(8,128)(2,1)S(1)}, u32[]{:S(2)}) copy-start(bf16[4,324,128]{2,1,0:T(8,128)(2,1)S(1)} %all-to-all-done.1.refs_1_) | copy-start | bytes 995332
where the time goes:
time: 61.8 us; the launch traced here: 61.2 us
  Pallas kernels  23.4 us (38%)
  starting transfers between devices  19.8 us (32%)
  local copies, waits for them, and re-layouts  9.02 us (15%)
  waiting for transfers between devices  8.3 us (13%)
  between operations  0.71 us (1%)
    pallas_call x1, Pallas kernels, per_device(): pl.pallas_call(nulls_kernel, out_shape=(vectors,) * 3, in_specs=[smem(),...  7.78 us
    ppermute x1, waiting for transfers between devices, per_device(): from_up = lax.ppermute(to_dn, 'chan', down)  5.34 us
    unnamed x16, local copies, waits for them, and re-layouts  5.2 us
    pallas_call x1, Pallas kernels, per_device(): pl.pallas_call(functools.partial(next_beams_kernel, dims), grid=(1,), out...  4.9 us
    ppermute x1, starting transfers between devices, per_device(): from_dn = lax.ppermute(to_up, 'chan', up)  4.81 us
    ppermute x1, starting transfers between devices, per_device(): sat_dn = lax.ppermute(sat_index, 'chan', up)  4.72 us
    pallas_call x1, Pallas kernels, per_device(): pl.pallas_call(functools.partial(first_beams_kernel, dims), grid=(1,), ou...  4.51 us
    all_to_all x1, starting transfers between devices, per_device(): lax.all_to_all(first, 'section', split_axis=0, concat_axis=0, tiled=True)  4.27 us
  transfers between devices with their start and end apart: 6, of which 4 were waited for; matrix products, arithmetic and copies ran while one was open for 4% of the time, Pallas kernels for 27%

commit v1 on v0

--- a/solution.py
+++ b/solution.py
@@ -7,10 +7,24 @@
 from jax.experimental.pallas import tpu as pltpu
 from jax.sharding import PartitionSpec as P
 
+
 LOADING = 100.0
 F32 = jnp.float32
 BF16 = jnp.bfloat16
 SUB = 8
+VMEM_GRANT = 20 * 1024 * 1024
+
+
+def partner(index, step, count):
+    if count & (count - 1) == 0:
+        return index ^ step
+    return lax.rem(index + step, count)
+
+
+def source_of(index, step, count):
+    if count & (count - 1) == 0:
+        return index ^ step
+    return lax.rem(index + count - step, count)
 
 
 def rounded_up(size):
@@ -66,32 +80,48 @@
 
 
 def stage_rows(dims):
-    groups, chans, group_beams, dishes, pad_beams = dims
+    _, chans, group_beams, dishes, _ = dims
     return rounded_up(chans * group_beams * 2 * dishes)
 
 
-def flush_beams(stage, out, dims):
-    groups = dims[0]
-    rows = out.shape[1]
-    for g in range(groups):
-        first = g * stage_rows(dims)
-        out[g] = stage[first : first + rows, :].astype(BF16)
-
-
-def first_beams_kernel(dims, x_ref, w_ref, out_ref, stage):
+def flush_beams(stage, outs, dims):
+    me = lax.axis_index("section")
+    rows = outs[0].shape[0]
+    for k, out in enumerate(outs):
+        first = pl.multiple_of(partner(me, k, dims[0]) * stage_rows(dims), SUB)
+        out[...] = stage[pl.ds(first, stage_rows(dims)), :][:rows].astype(BF16)
+
+
+def weight_rows_of(w_ref, d, pad_beams):
+    parts, _, chans, beams, ports = w_ref.shape
+    pieces = []
+    for part in range(parts):
+        for f in range(chans):
+            pieces.append(w_ref[part, d, f].astype(F32))
+            if pad_beams > beams:
+                pieces.append(jnp.zeros((pad_beams - beams, ports), F32))
+    return jnp.concatenate(pieces)
+
+
+def first_beams_kernel(dims, x_ref, w_ref, *refs):
+    outs, stage = refs[:-1], refs[-1]
     dishes = x_ref.shape[2]
-    chans = dims[1]
+    chans, pad_beams = dims[1], dims[4]
     ports = w_ref.shape[-1]
     spread = spread_matrix(ports, chans)
-    keep = own_channel(w_ref.shape[1], dims[4], ports, chans)
+    keep = own_channel(2 * chans * pad_beams, pad_beams, ports, chans)
     for d in range(dishes):
-        rows = beams_of(w_ref[d], spread, keep, x_ref[0, 0, d], x_ref[0, 1, d])
-        put_beams(rows, stage, d, dims)
-    flush_beams(stage, out_ref, dims)
-
-
-def nulls_kernel(sat_ref, sat_dn_ref, sat_up_ref, off_ref, ang_ref, x_ref,
-                 own_ref, dn_ref, up_ref, phase, folded):
+        rows = weight_rows_of(w_ref, d, pad_beams).astype(BF16)
+        put_beams(beams_of(rows, spread, keep, x_ref[0, 0, d], x_ref[0, 1, d]), stage, d, dims)
+    flush_beams(stage, outs, dims)
+
+
+def even_place():
+    return lax.rem(lax.axis_index("chan"), 2) == 0
+
+
+def nulls_kernel(sat_ref, sat_a_ref, sat_b_ref, off_ref, ang_ref, x_ref,
+                 own_ref, a_ref, b_ref, phase, folded):
     cycles, _, dishes, wide, samples = x_ref.shape
     ports = ang_ref.shape[-1]
     chans = wide // ports
@@ -99,25 +129,27 @@
     per_chan = 2 * slots
     rows = chans * per_chan
     spread = spread_matrix(ports, chans)
-    lane_t = lax.broadcasted_iota(jnp.int32, (1, samples), 1)
+    even = even_place()
+    place = lax.axis_index("chan")
+    last_place = lax.axis_size("chan") - 1
+    time = lax.broadcasted_iota(jnp.int32, (samples, off_ref.shape[1]), 0)
+    ones = jnp.ones((rows, off_ref.shape[1]), BF16)
     for c in range(cycles):
         for f in range(chans):
-            beside = sat_dn_ref if f == 0 else sat_up_ref
+            swapped = even if f == 0 else jnp.logical_not(even)
             for s in range(slots):
                 base = f * per_chan + s
                 phase[pl.ds(c * rows + base, 1), :] = ang_ref[pl.ds(sat_ref[c, s], 1), :]
                 phase[pl.ds(c * rows + base + slots, 1), :] = ang_ref[
-                    pl.ds(beside[c, s], 1), :
+                    pl.ds(jnp.where(swapped, sat_b_ref[c, s], sat_a_ref[c, s]), 1), :
                 ]
     angle = phase[...]
     cosine, sine = jnp.cos(angle), jnp.sin(angle)
     keep4 = own_channel(4 * rows, per_chan, ports, chans)
     keep2 = own_channel(2 * rows, per_chan, ports, chans)
     for c in range(cycles):
-        def count(j, total):
-            return total + jnp.where(lane_t == off_ref[c, j], 1.0, 0.0)
-
-        counts = lax.fori_loop(0, off_ref.shape[1], count, jnp.zeros((1, samples), F32), unroll=8)
+        hits = jnp.where(time == off_ref[c : c + 1, :], 1.0, 0.0).astype(BF16)
+        counts = dot_t(ones, hits)
         a_real = cosine[c * rows : (c + 1) * rows]
         a_imag = sine[c * rows : (c + 1) * rows]
         real_h, real_l = split(a_real)
@@ -160,8 +192,10 @@
                 last = (chans - 1) * per_chan + slots
                 where = slice(part * slots, (part + 1) * slots)
                 own_ref[c, d, where, :] = own + LOADING * along
-                dn_ref[c, d, where, :] = block[slots : 2 * slots]
-                up_ref[c, d, where, :] = block[last : last + slots]
+                to_dn = jnp.where(place > 0, block[slots : 2 * slots], 0.0)
+                to_up = jnp.where(place < last_place, block[last : last + slots], 0.0)
+                a_ref[c, d, where, :] = jnp.where(even, to_up, to_dn)
+                b_ref[c, d, where, :] = jnp.where(even, to_dn, to_up)
 
 
 def null_rows(rows, own, beside, chans, pad_beams):
@@ -185,29 +219,52 @@
     return jnp.concatenate(reals + imags)
 
 
-def next_beams_kernel(dims, x_ref, w_ref, own_ref, dn_ref, up_ref, out_ref, next_ref, stage):
+def beside_of(a_ref, b_ref, cycle, d):
+    even = even_place()
+    a, b = a_ref[cycle, d], b_ref[cycle, d]
+    return jnp.where(even, b, a), jnp.where(even, a, b)
+
+
+def next_beams_kernel(dims, cycle, x_ref, w_ref, own_ref, a_ref, b_ref, *refs):
+    outs, next_ref, stage = refs[:-2], refs[-2], refs[-1]
     dishes = x_ref.shape[2]
     chans, pad_beams = dims[1], dims[4]
     ports = w_ref.shape[-1]
     spread = spread_matrix(ports, chans)
-    keep = own_channel(w_ref.shape[1], pad_beams, ports, chans)
+    keep = own_channel(2 * chans * pad_beams, pad_beams, ports, chans)
     for d in range(dishes):
         rows = null_rows(
-            w_ref[d].astype(F32), own_ref[0, d], (dn_ref[0, d], up_ref[0, d]), chans, pad_beams
+            weight_rows_of(w_ref, d, pad_beams),
+            own_ref[cycle, d],
+            beside_of(a_ref, b_ref, cycle, d),
+            chans,
+            pad_beams,
         ).astype(BF16)
         next_ref[d] = rows
         put_beams(
-            beams_of(rows, spread, keep, x_ref[0, 0, d], x_ref[0, 1, d]), stage, d, dims
+            beams_of(rows, spread, keep, x_ref[cycle + 1, 0, d], x_ref[cycle + 1, 1, d]),
+            stage,
+            d,
+            dims,
         )
-    flush_beams(stage, out_ref, dims)
-
-
-def last_nulls_kernel(dims, w_ref, own_ref, dn_ref, up_ref, next_ref):
+    flush_beams(stage, outs, dims)
+
+
+def last_nulls_kernel(dims, cycle, w_ref, own_ref, a_ref, b_ref, out_ref):
     chans, pad_beams = dims[1], dims[4]
+    beams = out_ref.shape[3]
     for d in range(w_ref.shape[0]):
-        next_ref[d] = null_rows(
-            w_ref[d].astype(F32), own_ref[0, d], (dn_ref[0, d], up_ref[0, d]), chans, pad_beams
-        ).astype(BF16)
+        rows = null_rows(
+            w_ref[d].astype(F32),
+            own_ref[cycle, d],
+            beside_of(a_ref, b_ref, cycle, d),
+            chans,
+            pad_beams,
+        )
+        for part in range(2):
+            for f in range(chans):
+                first = (part * chans + f) * pad_beams
+                out_ref[part, d, f] = rows[first : first + beams].astype(BF16)
 
 
 def correlate_kernel(dims, scale, *refs):
@@ -220,23 +277,26 @@
     samples = gathered.shape[-1]
     block = 2 * dishes
     filler = jnp.zeros((pad_dishes, samples), F32)
-    for i in range(len(beam_refs) * pairs * 2):
+    for i in range(len(beam_refs) // groups * pairs * 2):
         gathered[i] = filler
-    for i, beam_ref in enumerate(beam_refs):
-        for g in range(groups):
-            values = beam_ref[g].astype(F32)
+    me = lax.axis_index("section")
+    cycles = len(beam_refs) // groups
+    for i in range(cycles):
+        for k in range(groups):
+            values = beam_refs[i * groups + k][...].astype(F32)
+            start = source_of(me, k, groups) * dishes
             for f in range(chans):
                 for b in range(group_beams):
                     for part in range(2):
                         first = (f * group_beams + b) * block + part * dishes
                         gathered[
                             (i * pairs + b * chans + f) * 2 + part,
-                            g * dishes : (g + 1) * dishes,
+                            pl.ds(start, dishes),
                             :,
                         ] = values[first : first + dishes]
     for pair in range(pairs):
         total = None
-        for i in range(len(beam_refs)):
+        for i in range(cycles):
             real = gathered[(i * pairs + pair) * 2]
             imag = gathered[(i * pairs + pair) * 2 + 1]
             top = jnp.concatenate([real, imag], axis=1)
@@ -253,7 +313,8 @@
             first = (part * pad_dishes + d) * pad_pairs
             pieces.append(sums[first : first + pad_pairs, 0:all_dishes])
         flat = jnp.concatenate(pieces, axis=1)
-        out_ref[part] = flat[:pairs]
+        for b in range(group_beams):
+            out_ref[part, b] = flat[b * chans : (b + 1) * chans]
 
 
 def vmem():
@@ -272,95 +333,99 @@
     peers = lax.axis_size("chan")
     group_beams = beams // groups
     pad_beams = rounded_up(beams)
+    assert cycles == 2 and chans == 2 and sat_index.shape[1] == 1
     dims = (groups, chans, group_beams, dishes, pad_beams)
     wide = ports * chans
     x = voltages.transpose(0, 1, 2, 4, 3, 5).reshape(cycles, 2, dishes, wide, samples)
-    w = jnp.pad(weights, ((0, 0), (0, 0), (0, 0), (0, pad_beams - beams), (0, 0)))
-    w = w.transpose(1, 0, 2, 3, 4).reshape(dishes, 2 * chans * pad_beams, ports)
-
-    up = [(i, i + 1) for i in range(peers - 1)]
-    down = [(i + 1, i) for i in range(peers - 1)]
-    sat_dn = lax.ppermute(sat_index, "chan", up)
-    sat_up = lax.ppermute(sat_index, "chan", down)
+
+    def pairs_of(first):
+        swaps = []
+        for i in range(peers):
+            other = i + 1 if i % 2 == first else i - 1
+            swaps.append((i, other if 0 <= other < peers else i))
+        return swaps
+
+    def params(**more):
+        return pltpu.CompilerParams(vmem_limit_bytes=VMEM_GRANT, **more)
+
+    def exchange(chunks):
+        got = [chunks[0]]
+        for k in range(1, groups):
+            path = [(i, int(partner(i, k, groups))) for i in range(groups)]
+            got.append(lax.ppermute(chunks[k], "section", path))
+        return got
+
+    sat_a = lax.ppermute(sat_index, "chan", pairs_of(0))
+    sat_b = lax.ppermute(sat_index, "chan", pairs_of(1))
 
     chunk = 2 * chans * group_beams * dishes
-    sent = jax.ShapeDtypeStruct((groups, chunk, samples), BF16)
+    sent = (jax.ShapeDtypeStruct((chunk, samples), BF16),) * groups
     stage = pltpu.VMEM((groups * stage_rows(dims), samples), F32)
-    w_rows = w.shape[1]
-
-    def x_of(cycle):
-        return pl.BlockSpec((1, 2, dishes, wide, samples), lambda i: (cycle, 0, 0, 0, 0))
-
-    def whole(*shape):
-        return pl.BlockSpec(shape, lambda i: (0,) * len(shape))
 
     first = pl.pallas_call(
         functools.partial(first_beams_kernel, dims),
-        grid=(1,),
         out_shape=sent,
-        in_specs=[x_of(0), whole(*w.shape)],
-        out_specs=whole(*sent.shape),
+        in_specs=[vmem()] * 2,
+        out_specs=(vmem(),) * groups,
         scratch_shapes=[stage],
+        compiler_params=params(),
         name="first_beams",
-    )(x, w)
-    first_all = lax.all_to_all(first, "section", split_axis=0, concat_axis=0, tiled=True)
+    )(x, weights)
+    first_all = exchange(first)
 
     rows = chans * 2 * slots
     vectors = jax.ShapeDtypeStruct((cycles, dishes, 2 * slots, ports), F32)
-    own, to_dn, to_up = pl.pallas_call(
+    own, to_a, to_b = pl.pallas_call(
         nulls_kernel,
         out_shape=(vectors,) * 3,
-        in_specs=[smem(), smem(), smem(), smem(), vmem(), vmem()],
+        in_specs=[smem(), smem(), smem(), vmem(), vmem(), vmem()],
         out_specs=(vmem(),) * 3,
         scratch_shapes=[
             pltpu.VMEM((cycles * rows, ports), F32),
             pltpu.VMEM((cycles * dishes * 2 * rows, wide), F32),
         ],
+        compiler_params=params(),
         name="nulls",
-    )(sat_index[:, 0], sat_dn[:, 0], sat_up[:, 0], offsets, angles, x)
-    from_up = lax.ppermute(to_dn, "chan", down)
-    from_dn = lax.ppermute(to_up, "chan", up)
-
-    def vec_of(cycle):
-        return pl.BlockSpec((1, dishes, 2 * slots, ports), lambda i: (cycle, 0, 0, 0))
-
-    second, w_next = pl.pallas_call(
-        functools.partial(next_beams_kernel, dims),
-        grid=(1,),
-        out_shape=(sent, jax.ShapeDtypeStruct(w.shape, BF16)),
-        in_specs=[x_of(1), whole(*w.shape), vec_of(0), vec_of(0), vec_of(0)],
-        out_specs=(whole(*sent.shape), whole(*w.shape)),
+    )(sat_index[:, 0], sat_a[:, 0], sat_b[:, 0], offsets, angles, x)
+    from_a = lax.ppermute(to_a, "chan", pairs_of(0))
+    from_b = lax.ppermute(to_b, "chan", pairs_of(1))
+
+    next_rows = jax.ShapeDtypeStruct((dishes, 2 * chans * pad_beams, ports), BF16)
+    *second, w_next = pl.pallas_call(
+        functools.partial(next_beams_kernel, dims, 0),
+        out_shape=(*sent, next_rows),
+        in_specs=[vmem()] * 5,
+        out_specs=(vmem(),) * (groups + 1),
         scratch_shapes=[stage],
+        compiler_params=params(),
         name="next_beams",
-    )(x, w, own, from_dn, from_up)
-    second_all = lax.all_to_all(second, "section", split_axis=0, concat_axis=0, tiled=True)
-
-    w_last = pl.pallas_call(
-        functools.partial(last_nulls_kernel, dims),
-        grid=(1,),
-        out_shape=jax.ShapeDtypeStruct(w.shape, BF16),
-        in_specs=[whole(*w.shape), vec_of(1), vec_of(1), vec_of(1)],
-        out_specs=whole(*w.shape),
+    )(x, weights, own, from_a, from_b)
+    second_all = exchange(second)
+
+    new_weights = pl.pallas_call(
+        functools.partial(last_nulls_kernel, dims, 1),
+        out_shape=jax.ShapeDtypeStruct(weights.shape, BF16),
+        in_specs=[vmem()] * 4,
+        out_specs=vmem(),
+        compiler_params=params(),
         name="last_nulls",
-    )(w_next, own, from_dn, from_up)
-    new_weights = w_last.reshape(dishes, 2, chans, pad_beams, ports)[:, :, :, :beams]
-    new_weights = new_weights.transpose(1, 0, 2, 3, 4)
+    )(w_next, own, from_a, from_b)
 
     all_dishes = dishes * groups
     pairs = group_beams * chans
     pad_dishes = rounded_up(all_dishes)
     vis = pl.pallas_call(
         functools.partial(correlate_kernel, dims, 1.0 / (cycles * samples)),
-        out_shape=jax.ShapeDtypeStruct((2, pairs, all_dishes * all_dishes), F32),
-        in_specs=[vmem(), vmem()],
+        out_shape=jax.ShapeDtypeStruct((2, group_beams, chans, all_dishes * all_dishes), F32),
+        in_specs=[vmem()] * (2 * groups),
         out_specs=vmem(),
         scratch_shapes=[
             pltpu.VMEM((cycles * pairs * 2, pad_dishes, samples), F32),
             pltpu.VMEM((2 * pad_dishes * rounded_up(pairs), samples), F32),
         ],
+        compiler_params=params(),
         name="correlate",
-    )(first_all, second_all)
-    vis = vis.reshape(2, group_beams, chans, all_dishes * all_dishes)
+    )(*first_all, *second_all)
     return vis, new_weights
 
 

time: 61.8 us -> 37.9 us (0.61)
  the two profiles are of different devices: /device:TPU:0 before, /device:TPU:21 now
where the time goes in v1:
time: 37.9 us; the launch traced here: 37.7 us
  starting transfers between devices  16.3 us (43%)
  Pallas kernels  12.7 us (34%)
  local copies, waits for them, and re-layouts  4.56 us (12%)
  waiting for transfers between devices  3.45 us (9%)
  between operations  0.73 us (2%)
    ppermute x6, starting transfers between devices, exchange(): got.append(lax.ppermute(chunks[k], 'section', path))  8.5 us
    pallas_call x1, Pallas kernels, per_device(): pl.pallas_call(nulls_kernel, out_shape=(vectors,) * 3, in_specs=[smem(),...  4.97 us
    unnamed x10, local copies, waits for them, and re-layouts  4.56 us
    ppermute x1, starting transfers between devices, per_device(): sat_b = lax.ppermute(sat_index, 'chan', pairs_of(1))  3 us
    pallas_call x1, Pallas kernels, per_device(): pl.pallas_call(functools.partial(next_beams_kernel, dims, 0), out_shape=(...  2.46 us
    pallas_call x1, Pallas kernels, per_device(): pl.pallas_call(functools.partial(first_beams_kernel, dims), out_shape=sen...  2.16 us
    ppermute x1, starting transfers between devices, per_device(): from_b = lax.ppermute(to_b, 'chan', pairs_of(1))  1.91 us
    pallas_call x1, Pallas kernels, per_device(): pl.pallas_call(functools.partial(correlate_kernel, dims, 1.0 / (cycles *...  1.62 us
  transfers between devices with their start and end apart: 10, of which 4 were waited for; matrix products, arithmetic and copies ran while one was open for 4% of the time, Pallas kernels for 24%

profile of v1, /device:TPU:21, one launch (start us, length us, event | category | flops | bytes accessed | tf_op | source)
XLA Modules:
  0.0 37.7 jit_solution(16555638293653958878)
XLA Ops:
  0.6 0.0 copy-start.2
  0.6 0.0 copy-start.1
  0.7 1.2 %copy.7.w_ref = bf16[2,9,2,36,188]{4,3,2,1,0:T(8,128)(2,1)S(1)} copy(bf16[2,9,2,36,188]{4,2,3,1,0:T(2,128)(2,1)} %param.6) | data formatting | bytes 974592 | tf_op args[1]
  1.9 0.0 copy-start
  1.9 2.0 %copy-done = bf16[2,2,9,2,188,128]{5,3,4,2,1,0:T(2,128)(2,1)S(1)} copy-done((bf16[2,2,9,2,188,128]{5,3,4,2,1,0:T(2,128)(2,1)S(1)}, bf16[2,2,9,2,188,128]{5,3,4,2,1,0:T(2,128)(2,1)}, u32[]{:S(2)}) %copy-start) | copy-done | bytes 3465240
  3.9 2.2 %first_beams.1 = (bf16[324,128]{1,0:T(8,128)(2,1)S(1)}, bf16[324,128]{1,0:T(8,128)(2,1)S(1)}, bf16[324,128]{1,0:T(8,128)(2,1)S(1)}, bf16[324,128]{1,0:T(8,128)(2,1)S(1)}) custom-call(bf16[2,2,9,376,128]{4,3,2,1,0:T(8,128)(2,1)S(1)} %bitcast.6, bf16[2,9,2,36,188]{4,3,2,1,0:T(8,128)(2,1)S(1)} %copy.7.w_ref), custom_call_target="tpu_custom_call" | custom-call | tf_op jit(solution)/shard_map/first_beams/pallas_call | solution.py:365
  6.0 0.7 %collective-permute-start = (bf16[324,128]{1,0:T(8,128)(2,1)S(1)}, bf16[324,128]{1,0:T(8,128)(2,1)S(1)}, u32[]{:S(2)}, u32[]{:S(2)}) collective-permute-start(bf16[324,128]{1,0:T(8,128)(2,1)S(1)} %get-tuple-element.15), channel_id=1, source_target_pairs={{0,1},{1,0},{2,3},{3,2},{4,5},{5,4},{6,7},{7,6},{8,9},{9,8},{10,11... | collective-permute-start | bytes 248840 | tf_op jit(solution)/shard_map/ppermute | solution.py:355
  6.8 3.0 %collective-permute-start.4 = (s32[2,1,2]{2,1,0:T(1,128)S(1)}, s32[2,1,2]{2,1,0:T(1,128)S(1)}, u32[]{:S(2)}, u32[]{:S(2)}) collective-permute-start(s32[2,1,2]{2,1,0:T(1,128)S(1)} %copy-done.2), channel_id=1, source_target_pairs={{0,0},{4,8},{8,4},{12,16},{16,12},{20,24},{24,20},{28,28},{1,1},{5... | collective-permute-start | bytes 56 | tf_op jit(solution)/shard_map/ppermute | solution.py:359
  9.8 1.4 %collective-permute-start.3 = (s32[2,1,2]{2,1,0:T(1,128)S(1)}, s32[2,1,2]{2,1,0:T(1,128)S(1)}, u32[]{:S(2)}, u32[]{:S(2)}) collective-permute-start(s32[2,1,2]{2,1,0:T(1,128)S(1)} %copy-done.2), channel_id=1, source_target_pairs={{0,4},{4,0},{8,12},{12,8},{16,20},{20,16},{24,28},{28,24},{1,5},{5... | collective-permute-start | bytes 56 | tf_op jit(solution)/shard_map/ppermute | solution.py:358
  11.2 0.8 %collective-permute-done.4 = s32[2,1,2]{2,1,0:T(1,128)S(1)} collective-permute-done((s32[2,1,2]{2,1,0:T(1,128)S(1)}, s32[2,1,2]{2,1,0:T(1,128)S(1)}, u32[]{:S(2)}, u32[]{:S(2)}) %collective-permute-start.4) | collective-permute-done | bytes 48 | tf_op jit(solution)/shard_map/ppermute | solution.py:359
  12.0 0.6 %collective-permute-done.3 = s32[2,1,2]{2,1,0:T(1,128)S(1)} collective-permute-done((s32[2,1,2]{2,1,0:T(1,128)S(1)}, s32[2,1,2]{2,1,0:T(1,128)S(1)}, u32[]{:S(2)}, u32[]{:S(2)}) %collective-permute-start.3) | collective-permute-done | bytes 48 | tf_op jit(solution)/shard_map/ppermute | solution.py:358
  12.6 0.0 copy-done.1
  12.6 5.0 %nulls.1 = (f32[2,9,4,188]{3,2,1,0:T(4,128)S(1)}, f32[2,9,4,188]{3,2,1,0:T(4,128)S(1)}, f32[2,9,4,188]{3,2,1,0:T(4,128)S(1)}) custom-call(s32[2,2]{1,0:T(2,128)S(1)} %bitcast.9, s32[2,2]{1,0:T(2,128)S(1)} %bitcast.11, s32[2,2]{1,0:T(2,128)S(1)} %bitcast.10, s32[2,128]{1,0:T(2,128)S(1)} %copy-done.3, f32[64,188]{1,0:T(8,128)S(1)} %copy-done.1, ...), custom_call_target="tpu_custom_call" | custom-call | tf_op jit(solution)/shard_map/nulls/pallas_call | solution.py:378
  17.6 1.4 %collective-permute-start.5 = (f32[2,9,4,188]{3,2,1,0:T(4,128)S(1)}, f32[2,9,4,188]{3,2,1,0:T(4,128)S(1)}, u32[]{:S(2)}, u32[]{:S(2)}) collective-permute-start(f32[2,9,4,188]{3,2,1,0:T(4,128)S(1)} %get-tuple-element.19), channel_id=1, source_target_pairs={{0,4},{4,0},{8,12},{12,8},{16,20},{20,16},{24,28},{28,24},{1,5},{5... | collective-permute-start | bytes 162440 | tf_op jit(solution)/shard_map/ppermute | solution.py:390
  19.0 1.9 %collective-permute-start.6 = (f32[2,9,4,188]{3,2,1,0:T(4,128)S(1)}, f32[2,9,4,188]{3,2,1,0:T(4,128)S(1)}, u32[]{:S(2)}, u32[]{:S(2)}) collective-permute-start(f32[2,9,4,188]{3,2,1,0:T(4,128)S(1)} %get-tuple-element.20), channel_id=1, source_target_pairs={{0,0},{4,8},{8,4},{12,16},{16,12},{20,24},{24,20},{28,28},{1,1},{5... | collective-permute-start | bytes 162440 | tf_op jit(solution)/shard_map/ppermute | solution.py:391
  20.9 0.3 collective-permute-start.1
  21.2 3.1 %collective-permute-start.2 = (bf16[324,128]{1,0:T(8,128)(2,1)S(1)}, bf16[324,128]{1,0:T(8,128)(2,1)S(1)}, u32[]{:S(2)}, u32[]{:S(2)}) collective-permute-start(bf16[324,128]{1,0:T(8,128)(2,1)S(1)} %get-tuple-element.17), channel_id=1, source_target_pairs={{0,3},{1,2},{2,1},{3,0},{4,7},{5,6},{6,5},{7,4},{8,11},{9,10},{10,... | collective-permute-start | bytes 248840 | tf_op jit(solution)/shard_map/ppermute | solution.py:355
  24.3 0.0 collective-permute-done.5.a_ref
  24.3 0.7 %collective-permute-done.6.b_ref = f32[2,9,4,188]{3,2,1,0:T(4,128)S(1)} collective-permute-done((f32[2,9,4,188]{3,2,1,0:T(4,128)S(1)}, f32[2,9,4,188]{3,2,1,0:T(4,128)S(1)}, u32[]{:S(2)}, u32[]{:S(2)}) %collective-permute-start.6) | collective-permute-done | bytes 54176 | tf_op jit(solution)/shard_map/ppermute | solution.py:391
  25.0 2.5 %next_beams.1 = (bf16[324,128]{1,0:T(8,128)(2,1)S(1)}, bf16[324,128]{1,0:T(8,128)(2,1)S(1)}, bf16[324,128]{1,0:T(8,128)(2,1)S(1)}, bf16[324,128]{1,0:T(8,128)(2,1)S(1)}, bf16[9,160,188]{2,1,0:T(8,128)(2,1)S(1)}) custom-call(bf16[2,2,9,376,128]{4,3,2,1,0:T(8,128)(2,1)S(1)} %bitcast.8, bf16[2,9,2,36,188]{4,3,2,1,0:T(8,128)(2,1)S(1)} %copy.7.w_ref, ...), custom_call_target="tpu_custom_call" | custom-call | tf_op jit(solution)/shard_map/next_beams/pallas_call | solution.py:394
  27.4 2.7 %collective-permute-start.7 = (bf16[324,128]{1,0:T(8,128)(2,1)S(1)}, bf16[324,128]{1,0:T(8,128)(2,1)S(1)}, u32[]{:S(2)}, u32[]{:S(2)}) collective-permute-start(bf16[324,128]{1,0:T(8,128)(2,1)S(1)} %get-tuple-element.22), channel_id=1, source_target_pairs={{0,1},{1,0},{2,3},{3,2},{4,5},{5,4},{6,7},{7,6},{8,9},{9,8},{10,11... | collective-permute-start | bytes 248840 | tf_op jit(solution)/shard_map/ppermute | solution.py:355
  30.1 0.2 collective-permute-start.8
  30.3 0.0 collective-permute-done.refs_1_
  30.3 1.5 %collective-permute-start.9 = (bf16[324,128]{1,0:T(8,128)(2,1)S(1)}, bf16[324,128]{1,0:T(8,128)(2,1)S(1)}, u32[]{:S(2)}, u32[]{:S(2)}) collective-permute-start(bf16[324,128]{1,0:T(8,128)(2,1)S(1)} %get-tuple-element.24), channel_id=1, source_target_pairs={{0,3},{1,2},{2,1},{3,0},{4,7},{5,6},{6,5},{7,4},{8,11},{9,10},{10,... | collective-permute-start | bytes 248840 | tf_op jit(solution)/shard_map/ppermute | solution.py:355
  31.8 1.5 %last_nulls.1 = bf16[2,9,2,36,188]{4,3,2,1,0:T(8,128)(2,1)S(1)} custom-call(bf16[9,160,188]{2,1,0:T(8,128)(2,1)S(1)} %get-tuple-element.25.w_ref, f32[2,9,4,188]{3,2,1,0:T(4,128)S(1)} %get-tuple-element.18.own_ref, f32[2,9,4,188]{3,2,1,0:T(4,128)S(1)} %collective-permute-done.5.a_ref, f32[2,9,4,188]{3,2,1,0:T(4,128)S(1)} %collective-permute-done.6.b_ref), custom_call_target="tpu_custom_call" | custom-call | tf_op jit(solution)/shard_map/last_nulls/pallas_call | solution.py:405
  33.3 1.4 %copy.9 = bf16[2,9,2,36,188]{4,2,3,1,0:T(2,128)(2,1)} copy(bf16[2,9,2,36,188]{4,3,2,1,0:T(8,128)(2,1)S(1)} %last_nulls.1) | data formatting | bytes 974592
  34.7 0.0 collective-permute-done.1.refs_2_
  34.7 0.0 collective-permute-done.2.refs_3_
  34.7 0.0 collective-permute-done.7.refs_5_
  34.7 0.0 collective-permute-done.8.refs_6_
  34.7 1.4 %collective-permute-done.9.refs_7_ = bf16[324,128]{1,0:T(8,128)(2,1)S(1)} collective-permute-done((bf16[324,128]{1,0:T(8,128)(2,1)S(1)}, bf16[324,128]{1,0:T(8,128)(2,1)S(1)}, u32[]{:S(2)}, u32[]{:S(2)}) %collective-permute-start.9) | collective-permute-done | bytes 82976 | tf_op jit(solution)/shard_map/ppermute | solution.py:355
  36.1 1.6 %correlate.1 = f32[2,9,2,1296]{3,2,1,0:T(2,128)} custom-call(bf16[324,128]{1,0:T(8,128)(2,1)S(1)} %get-tuple-element.14.refs_0_, bf16[324,128]{1,0:T(8,128)(2,1)S(1)} %collective-permute-done.refs_1_, bf16[324,128]{1,0:T(8,128)(2,1)S(1)} %collective-permute-done.1.refs_2_, bf16[324,128]{1,0:T(8,128)(2,1)S(1)} %collective-permute-done.2.refs_3_, ...), custom_call_target="tpu_custom_call" | custom-call | tf_op jit(solution)/shard_map/correlate/pallas_call | solution.py:417
  (3 shorter events, 0.0 us)
Async XLA Ops:
  0.6 6.1 %copy-start.2 = (s32[2,1,2]{2,1,0:T(1,128)S(1)}, s32[2,1,2]{2,1,0:T(1,128)}, u32[]{:S(2)}) copy-start(s32[2,1,2]{2,1,0:T(1,128)} %param.7) | copy-start | bytes 52
  0.6 11.9 %copy-start.1 = (f32[64,188]{1,0:T(8,128)S(1)}, f32[64,188]{1,0:T(8,128)}, u32[]{:S(2)}) copy-start(f32[64,188]{1,0:T(8,128)} %ang_ref.1) | copy-start | bytes 144388
  0.7 11.9 %copy-start.3 = (s32[2,128]{1,0:T(2,128)S(1)}, s32[2,128]{1,0:T(2,128)}, u32[]{:S(2)}) copy-start(s32[2,128]{1,0:T(2,128)} %off_ref.1) | copy-start | bytes 3076
  1.9 2.0 %copy-start = (bf16[2,2,9,2,188,128]{5,3,4,2,1,0:T(2,128)(2,1)S(1)}, bf16[2,2,9,2,188,128]{5,3,4,2,1,0:T(2,128)(2,1)}, u32[]{:S(2)}) copy-start(bf16[2,2,9,2,188,128]{5,3,4,2,1,0:T(2,128)(2,1)} %param.5) | copy-start | bytes 10395652
  6.0 24.3 %collective-permute-start = (bf16[324,128]{1,0:T(8,128)(2,1)S(1)}, bf16[324,128]{1,0:T(8,128)(2,1)S(1)}, u32[]{:S(2)}, u32[]{:S(2)}) collective-permute-start(bf16[324,128]{1,0:T(8,128)(2,1)S(1)} %get-tuple-element.15), channel_id=1, source_target_pairs={{0,1},{1,0},{2,3},{3,2},{4,5},{5,4},{6,7},{7,6},{8,9},{9,8},{10,11... | collective-permute-start | bytes 248840 | tf_op jit(solution)/shard_map/ppermute | solution.py:355
  6.8 5.2 %collective-permute-start.4 = (s32[2,1,2]{2,1,0:T(1,128)S(1)}, s32[2,1,2]{2,1,0:T(1,128)S(1)}, u32[]{:S(2)}, u32[]{:S(2)}) collective-permute-start(s32[2,1,2]{2,1,0:T(1,128)S(1)} %copy-done.2), channel_id=1, source_target_pairs={{0,0},{4,8},{8,4},{12,16},{16,12},{20,24},{24,20},{28,28},{1,1},{5... | collective-permute-start | bytes 56 | tf_op jit(solution)/shard_map/ppermute | solution.py:359
  9.8 2.8 %collective-permute-start.3 = (s32[2,1,2]{2,1,0:T(1,128)S(1)}, s32[2,1,2]{2,1,0:T(1,128)S(1)}, u32[]{:S(2)}, u32[]{:S(2)}) collective-permute-start(s32[2,1,2]{2,1,0:T(1,128)S(1)} %copy-done.2), channel_id=1, source_target_pairs={{0,4},{4,0},{8,12},{12,8},{16,20},{20,16},{24,28},{28,24},{1,5},{5... | collective-permute-start | bytes 56 | tf_op jit(solution)/shard_map/ppermute | solution.py:358
  17.6 6.7 %collective-permute-start.5 = (f32[2,9,4,188]{3,2,1,0:T(4,128)S(1)}, f32[2,9,4,188]{3,2,1,0:T(4,128)S(1)}, u32[]{:S(2)}, u32[]{:S(2)}) collective-permute-start(f32[2,9,4,188]{3,2,1,0:T(4,128)S(1)} %get-tuple-element.19), channel_id=1, source_target_pairs={{0,4},{4,0},{8,12},{12,8},{16,20},{20,16},{24,28},{28,24},{1,5},{5... | collective-permute-start | bytes 162440 | tf_op jit(solution)/shard_map/ppermute | solution.py:390
  19.0 6.0 %collective-permute-start.6 = (f32[2,9,4,188]{3,2,1,0:T(4,128)S(1)}, f32[2,9,4,188]{3,2,1,0:T(4,128)S(1)}, u32[]{:S(2)}, u32[]{:S(2)}) collective-permute-start(f32[2,9,4,188]{3,2,1,0:T(4,128)S(1)} %get-tuple-element.20), channel_id=1, source_target_pairs={{0,0},{4,8},{8,4},{12,16},{16,12},{20,24},{24,20},{28,28},{1,1},{5... | collective-permute-start | bytes 162440 | tf_op jit(solution)/shard_map/ppermute | solution.py:391
  20.9 13.8 %collective-permute-start.1 = (bf16[324,128]{1,0:T(8,128)(2,1)S(1)}, bf16[324,128]{1,0:T(8,128)(2,1)S(1)}, u32[]{:S(2)}, u32[]{:S(2)}) collective-permute-start(bf16[324,128]{1,0:T(8,128)(2,1)S(1)} %get-tuple-element.16), channel_id=1, source_target_pairs={{0,2},{1,3},{2,0},{3,1},{4,6},{5,7},{6,4},{7,5},{8,10},{9,11},{10,... | collective-permute-start | bytes 248840 | tf_op jit(solution)/shard_map/ppermute | solution.py:355
  21.2 13.5 %collective-permute-start.2 = (bf16[324,128]{1,0:T(8,128)(2,1)S(1)}, bf16[324,128]{1,0:T(8,128)(2,1)S(1)}, u32[]{:S(2)}, u32[]{:S(2)}) collective-permute-start(bf16[324,128]{1,0:T(8,128)(2,1)S(1)} %get-tuple-element.17), channel_id=1, source_target_pairs={{0,3},{1,2},{2,1},{3,0},{4,7},{5,6},{6,5},{7,4},{8,11},{9,10},{10,... | collective-permute-start | bytes 248840 | tf_op jit(solution)/shard_map/ppermute | solution.py:355
  27.4 7.2 %collective-permute-start.7 = (bf16[324,128]{1,0:T(8,128)(2,1)S(1)}, bf16[324,128]{1,0:T(8,128)(2,1)S(1)}, u32[]{:S(2)}, u32[]{:S(2)}) collective-permute-start(bf16[324,128]{1,0:T(8,128)(2,1)S(1)} %get-tuple-element.22), channel_id=1, source_target_pairs={{0,1},{1,0},{2,3},{3,2},{4,5},{5,4},{6,7},{7,6},{8,9},{9,8},{10,11... | collective-permute-start | bytes 248840 | tf_op jit(solution)/shard_map/ppermute | solution.py:355
  30.1 4.6 %collective-permute-start.8 = (bf16[324,128]{1,0:T(8,128)(2,1)S(1)}, bf16[324,128]{1,0:T(8,128)(2,1)S(1)}, u32[]{:S(2)}, u32[]{:S(2)}) collective-permute-start(bf16[324,128]{1,0:T(8,128)(2,1)S(1)} %get-tuple-element.23), channel_id=1, source_target_pairs={{0,2},{1,3},{2,0},{3,1},{4,6},{5,7},{6,4},{7,5},{8,10},{9,11},{10,... | collective-permute-start | bytes 248840 | tf_op jit(solution)/shard_map/ppermute | solution.py:355
  30.3 5.8 %collective-permute-start.9 = (bf16[324,128]{1,0:T(8,128)(2,1)S(1)}, bf16[324,128]{1,0:T(8,128)(2,1)S(1)}, u32[]{:S(2)}, u32[]{:S(2)}) collective-permute-start(bf16[324,128]{1,0:T(8,128)(2,1)S(1)} %get-tuple-element.24), channel_id=1, source_target_pairs={{0,3},{1,2},{2,1},{3,0},{4,7},{5,6},{6,5},{7,4},{8,11},{9,10},{10,... | collective-permute-start | bytes 248840 | tf_op jit(solution)/shard_map/ppermute | solution.py:355

commit v2 on v1

--- a/solution.py
+++ b/solution.py
@@ -13,18 +13,6 @@
 BF16 = jnp.bfloat16
 SUB = 8
 VMEM_GRANT = 20 * 1024 * 1024
-
-
-def partner(index, step, count):
-    if count & (count - 1) == 0:
-        return index ^ step
-    return lax.rem(index + step, count)
-
-
-def source_of(index, step, count):
-    if count & (count - 1) == 0:
-        return index ^ step
-    return lax.rem(index + count - step, count)
 
 
 def rounded_up(size):
@@ -84,11 +72,11 @@
     return rounded_up(chans * group_beams * 2 * dishes)
 
 
-def flush_beams(stage, outs, dims):
+def flush_beams(stage, outs, steps, dims):
     me = lax.axis_index("section")
     rows = outs[0].shape[0]
-    for k, out in enumerate(outs):
-        first = pl.multiple_of(partner(me, k, dims[0]) * stage_rows(dims), SUB)
+    for k, out in zip(steps, outs):
+        first = pl.multiple_of((me ^ k) * stage_rows(dims), SUB)
         out[...] = stage[pl.ds(first, stage_rows(dims)), :][:rows].astype(BF16)
 
 
@@ -104,16 +92,23 @@
 
 
 def first_beams_kernel(dims, x_ref, w_ref, *refs):
-    outs, stage = refs[:-1], refs[-1]
+    (near, mine, *far), (stage, held, sems) = refs[:-3], refs[-3:]
     dishes = x_ref.shape[2]
     chans, pad_beams = dims[1], dims[4]
+    copies = []
+    for d in range(dishes):
+        copies.append(pltpu.make_async_copy(x_ref.at[0, :, d], held.at[:, d], sems.at[d]))
+        copies[d].start()
     ports = w_ref.shape[-1]
     spread = spread_matrix(ports, chans)
     keep = own_channel(2 * chans * pad_beams, pad_beams, ports, chans)
     for d in range(dishes):
         rows = weight_rows_of(w_ref, d, pad_beams).astype(BF16)
-        put_beams(beams_of(rows, spread, keep, x_ref[0, 0, d], x_ref[0, 1, d]), stage, d, dims)
-    flush_beams(stage, outs, dims)
+        copies[d].wait()
+        put_beams(beams_of(rows, spread, keep, held[0, d], held[1, d]), stage, d, dims)
+    flush_beams(stage, [mine, near], [0, 1], dims)
+    for i, out in enumerate(far):
+        flush_beams(stage, [out.at[0], out.at[1]], [2 * i + 2, 2 * i + 3], dims)
 
 
 def even_place():
@@ -225,8 +220,12 @@
     return jnp.where(even, b, a), jnp.where(even, a, b)
 
 
-def next_beams_kernel(dims, cycle, x_ref, w_ref, own_ref, a_ref, b_ref, *refs):
-    outs, next_ref, stage = refs[:-2], refs[-2], refs[-1]
+def next_beams_kernel(dims, cycle, x_ref, w_ref, own_ref, a_ref, b_ref, near_ref, *refs):
+    groups = dims[0]
+    passed, (near, mine, *far), (next_ref, stage) = refs[: groups // 2 - 1], refs[groups // 2 - 1 : -2], refs[-2:]
+    near[0] = near_ref[...]
+    for i, passed_ref in enumerate(passed):
+        near[i + 1] = passed_ref[1]
     dishes = x_ref.shape[2]
     chans, pad_beams = dims[1], dims[4]
     ports = w_ref.shape[-1]
@@ -247,7 +246,7 @@
             d,
             dims,
         )
-    flush_beams(stage, outs, dims)
+    flush_beams(stage, [mine, near.at[groups // 2], *far], range(groups), dims)
 
 
 def last_nulls_kernel(dims, cycle, w_ref, own_ref, a_ref, b_ref, out_ref):
@@ -277,23 +276,31 @@
     samples = gathered.shape[-1]
     block = 2 * dishes
     filler = jnp.zeros((pad_dishes, samples), F32)
-    for i in range(len(beam_refs) // groups * pairs * 2):
+    for i in range(gathered.shape[0]):
         gathered[i] = filler
     me = lax.axis_index("section")
-    cycles = len(beam_refs) // groups
-    for i in range(cycles):
-        for k in range(groups):
-            values = beam_refs[i * groups + k][...].astype(F32)
-            start = source_of(me, k, groups) * dishes
-            for f in range(chans):
-                for b in range(group_beams):
-                    for part in range(2):
-                        first = (f * group_beams + b) * block + part * dishes
-                        gathered[
-                            (i * pairs + b * chans + f) * 2 + part,
-                            pl.ds(start, dishes),
-                            :,
-                        ] = values[first : first + dishes]
+    cycles = 2
+    mine, near, far = beam_refs[:2], beam_refs[2], beam_refs[3:]
+    blocks = [(0, 0, mine[0].at[...]), (1, 0, mine[1].at[...])]
+    for i in range(groups // 2):
+        blocks.append((0, 2 * i + 1, near.at[i]))
+    blocks.append((1, 1, near.at[groups // 2]))
+    for i in range(groups // 2 - 1):
+        blocks.append((0, 2 * i + 2, far[i].at[0]))
+    for k in range(2, groups):
+        blocks.append((1, k, far[groups // 2 - 1 + k - 2].at[...]))
+    for i, k, beam_ref in blocks:
+        values = beam_ref[...].astype(F32)
+        start = (me ^ k) * dishes
+        for f in range(chans):
+            for b in range(group_beams):
+                for part in range(2):
+                    first = (f * group_beams + b) * block + part * dishes
+                    gathered[
+                        (i * pairs + b * chans + f) * 2 + part,
+                        pl.ds(start, dishes),
+                        :,
+                    ] = values[first : first + dishes]
     for pair in range(pairs):
         total = None
         for i in range(cycles):
@@ -334,44 +341,49 @@
     group_beams = beams // groups
     pad_beams = rounded_up(beams)
     assert cycles == 2 and chans == 2 and sat_index.shape[1] == 1
+    assert groups > 1 and groups & (groups - 1) == 0
     dims = (groups, chans, group_beams, dishes, pad_beams)
     wide = ports * chans
     x = voltages.transpose(0, 1, 2, 4, 3, 5).reshape(cycles, 2, dishes, wide, samples)
 
-    def pairs_of(first):
-        swaps = []
+    def swap(value, first):
+        path = []
         for i in range(peers):
             other = i + 1 if i % 2 == first else i - 1
-            swaps.append((i, other if 0 <= other < peers else i))
-        return swaps
+            for q in range(groups):
+                to = other * groups + q if 0 <= other < peers else i * groups + (q ^ 1)
+                path.append((i * groups + q, to))
+        return lax.ppermute(value, ("chan", "section"), path)
 
     def params(**more):
         return pltpu.CompilerParams(vmem_limit_bytes=VMEM_GRANT, **more)
 
-    def exchange(chunks):
-        got = [chunks[0]]
-        for k in range(1, groups):
-            path = [(i, int(partner(i, k, groups))) for i in range(groups)]
-            got.append(lax.ppermute(chunks[k], "section", path))
-        return got
-
-    sat_a = lax.ppermute(sat_index, "chan", pairs_of(0))
-    sat_b = lax.ppermute(sat_index, "chan", pairs_of(1))
+    def step_over(value, step):
+        return lax.ppermute(value, "section", [(i, i ^ step) for i in range(groups)])
+
+    sat_b = swap(sat_index, 1)
+    sat_a = swap(sat_index, 0)
 
     chunk = 2 * chans * group_beams * dishes
-    sent = (jax.ShapeDtypeStruct((chunk, samples), BF16),) * groups
+    piece = jax.ShapeDtypeStruct((chunk, samples), BF16)
+    two = jax.ShapeDtypeStruct((2, chunk, samples), BF16)
+    several = jax.ShapeDtypeStruct((groups // 2 + 1, chunk, samples), BF16)
     stage = pltpu.VMEM((groups * stage_rows(dims), samples), F32)
 
-    first = pl.pallas_call(
+    first_near, first_mine, *first_far = pl.pallas_call(
         functools.partial(first_beams_kernel, dims),
-        out_shape=sent,
-        in_specs=[vmem()] * 2,
-        out_specs=(vmem(),) * groups,
-        scratch_shapes=[stage],
+        out_shape=(piece, piece) + (two,) * (groups // 2 - 1),
+        in_specs=[pl.BlockSpec(memory_space=pltpu.HBM), vmem()],
+        out_specs=(vmem(),) * (groups // 2 + 1),
+        scratch_shapes=[
+            stage,
+            pltpu.VMEM((2, dishes, wide, samples), BF16),
+            pltpu.SemaphoreType.DMA((dishes,)),
+        ],
         compiler_params=params(),
         name="first_beams",
-    )(x, weights)
-    first_all = exchange(first)
+    )(pltpu.with_memory_space_constraint(x, pltpu.HBM), weights)
+    first_got = [step_over(value, 2 * i + 2) for i, value in enumerate(first_far)]
 
     rows = chans * 2 * slots
     vectors = jax.ShapeDtypeStruct((cycles, dishes, 2 * slots, ports), F32)
@@ -387,20 +399,21 @@
         compiler_params=params(),
         name="nulls",
     )(sat_index[:, 0], sat_a[:, 0], sat_b[:, 0], offsets, angles, x)
-    from_a = lax.ppermute(to_a, "chan", pairs_of(0))
-    from_b = lax.ppermute(to_b, "chan", pairs_of(1))
+    from_b = swap(to_b, 1)
+    from_a = swap(to_a, 0)
 
     next_rows = jax.ShapeDtypeStruct((dishes, 2 * chans * pad_beams, ports), BF16)
-    *second, w_next = pl.pallas_call(
+    second_near, second_mine, *second_far, w_next = pl.pallas_call(
         functools.partial(next_beams_kernel, dims, 0),
-        out_shape=(*sent, next_rows),
-        in_specs=[vmem()] * 5,
+        out_shape=(several, piece) + (piece,) * (groups - 2) + (next_rows,),
+        in_specs=[vmem()] * (5 + groups // 2),
         out_specs=(vmem(),) * (groups + 1),
         scratch_shapes=[stage],
         compiler_params=params(),
         name="next_beams",
-    )(x, weights, own, from_a, from_b)
-    second_all = exchange(second)
+    )(x, weights, own, from_a, from_b, first_near, *first_got)
+    second_got = [step_over(value, k + 2) for k, value in enumerate(second_far)]
+    near_got = step_over(second_near, 1)
 
     new_weights = pl.pallas_call(
         functools.partial(last_nulls_kernel, dims, 1),
@@ -417,7 +430,7 @@
     vis = pl.pallas_call(
         functools.partial(correlate_kernel, dims, 1.0 / (cycles * samples)),
         out_shape=jax.ShapeDtypeStruct((2, group_beams, chans, all_dishes * all_dishes), F32),
-        in_specs=[vmem()] * (2 * groups),
+        in_specs=[vmem()] * (3 + groups // 2 - 1 + groups - 2),
         out_specs=vmem(),
         scratch_shapes=[
             pltpu.VMEM((cycles * pairs * 2, pad_dishes, samples), F32),
@@ -425,7 +438,7 @@
         ],
         compiler_params=params(),
         name="correlate",
-    )(*first_all, *second_all)
+    )(first_mine, second_mine, near_got, *first_got, *second_got)
     return vis, new_weights
 
 

time: 37.9 us -> 36.1 us (0.953)
  the two profiles are of different devices: /device:TPU:21 before, /device:TPU:9 now
where the time goes in v2:
time: 36.1 us; the launch traced here: 35.9 us
  Pallas kernels  15.1 us (42%)
  starting transfers between devices  10.5 us (29%)
  waiting for transfers between devices  6.93 us (19%)
  local copies, waits for them, and re-layouts  2.71 us (8%)
  between operations  0.71 us (2%)
    ppermute x4, starting transfers between devices, step_over(): lax.ppermute(value, 'section', [(i, i ^ step) for i in range(groups)])  6.55 us
    ppermute x4, waiting for transfers between devices, swap(): return lax.ppermute(value, ('chan', 'section'), path)  5.49 us
    pallas_call x1, Pallas kernels, per_device(): pl.pallas_call(nulls_kernel, out_shape=(vectors,) * 3, in_specs=[smem(),...  4.97 us
    pallas_call x1, Pallas kernels, per_device(): pl.pallas_call(functools.partial(first_beams_kernel, dims), out_shape=(pi...  4.54 us
    ppermute x4, starting transfers between devices, swap(): return lax.ppermute(value, ('chan', 'section'), path)  3.93 us
    unnamed x10, local copies, waits for them, and re-layouts  2.71 us
    pallas_call x1, Pallas kernels, per_device(): pl.pallas_call(functools.partial(next_beams_kernel, dims, 0), out_shape=(...  2.49 us
    pallas_call x1, Pallas kernels, per_device(): pl.pallas_call(functools.partial(correlate_kernel, dims, 1.0 / (cycles *...  1.62 us
  transfers between devices with their start and end apart: 8, of which 5 were waited for; matrix products, arithmetic and copies ran while one was open for 4% of the time, Pallas kernels for 18%

profile of v2, /device:TPU:9, one launch (start us, length us, event | category | flops | bytes accessed | tf_op | source)
XLA Modules:
  0.0 35.9 jit_solution(17130207250546178565)
XLA Ops:
  0.6 0.0 copy-start
  0.6 0.0 copy-start.2
  0.7 0.0 copy-start.1
  0.7 0.0 copy-start.3
  0.7 1.3 %copy.7.w_ref = bf16[2,9,2,36,188]{4,3,2,1,0:T(8,128)(2,1)S(1)} copy(bf16[2,9,2,36,188]{4,2,3,1,0:T(2,128)(2,1)} %param.6) | data formatting | bytes 974592 | tf_op args[1]
  2.0 4.5 %first_beams.1 = (bf16[324,128]{1,0:T(8,128)(2,1)S(1)}, bf16[324,128]{1,0:T(8,128)(2,1)S(1)}, bf16[2,324,128]{2,1,0:T(8,128)(2,1)S(1)}) custom-call(bf16[2,2,9,376,128]{4,3,2,1,0:T(8,128)(2,1)} %bitcast.6, bf16[2,9,2,36,188]{4,3,2,1,0:T(8,128)(2,1)S(1)} %copy.7.w_ref), custom_call_target="tpu_custom_call" | custom-call | tf_op jit(solution)/shard_map/first_beams/pallas_call | solution.py:373
  6.6 1.3 %collective-permute-start.4 = (bf16[2,324,128]{2,1,0:T(8,128)(2,1)S(1)}, bf16[2,324,128]{2,1,0:T(8,128)(2,1)S(1)}, u32[]{:S(2)}, u32[]{:S(2)}) collective-permute-start(bf16[2,324,128]{2,1,0:T(8,128)(2,1)S(1)} %get-tuple-element.18), channel_id=1, source_target_pairs={{0,2},{1,3},{2,0},{3,1},{4,6},{5,7},{6,4},{7,5},{8,10},{9,11},{10,... | collective-permute-start | bytes 497672 | tf_op jit(solution)/shard_map/ppermute | solution.py:362
  7.9 0.0 copy-done.2
  7.9 1.1 %collective-permute-start.1 = (s32[2,1,2]{2,1,0:T(1,128)S(1)}, s32[2,1,2]{2,1,0:T(1,128)S(1)}, u32[]{:S(2)}, u32[]{:S(2)}) collective-permute-start(s32[2,1,2]{2,1,0:T(1,128)S(1)} %copy-done.2), channel_id=1, source_target_pairs={{0,1},{1,0},{2,3},{3,2},{4,8},{5,9},{6,10},{7,11},{8,4},{9,5},{10,... | collective-permute-start | bytes 56 | tf_op jit(solution)/shard_map/ppermute | solution.py:356
  9.0 1.4 %collective-permute-start = (s32[2,1,2]{2,1,0:T(1,128)S(1)}, s32[2,1,2]{2,1,0:T(1,128)S(1)}, u32[]{:S(2)}, u32[]{:S(2)}) collective-permute-start(s32[2,1,2]{2,1,0:T(1,128)S(1)} %copy-done.2), channel_id=1, source_target_pairs={{0,4},{1,5},{2,6},{3,7},{4,0},{5,1},{6,2},{7,3},{8,12},{9,13},{10,... | collective-permute-start | bytes 56 | tf_op jit(solution)/shard_map/ppermute | solution.py:356
  10.4 0.8 %collective-permute-done.1 = s32[2,1,2]{2,1,0:T(1,128)S(1)} collective-permute-done((s32[2,1,2]{2,1,0:T(1,128)S(1)}, s32[2,1,2]{2,1,0:T(1,128)S(1)}, u32[]{:S(2)}, u32[]{:S(2)}) %collective-permute-start.1) | collective-permute-done | bytes 48 | tf_op jit(solution)/shard_map/ppermute | solution.py:356
  11.2 0.5 %collective-permute-done = s32[2,1,2]{2,1,0:T(1,128)S(1)} collective-permute-done((s32[2,1,2]{2,1,0:T(1,128)S(1)}, s32[2,1,2]{2,1,0:T(1,128)S(1)}, u32[]{:S(2)}, u32[]{:S(2)}) %collective-permute-start) | collective-permute-done | bytes 48 | tf_op jit(solution)/shard_map/ppermute | solution.py:356
  11.7 0.0 copy-done
  11.7 0.0 copy-done.1
  11.7 0.0 copy-done.3
  11.7 5.0 %nulls.1 = (f32[2,9,4,188]{3,2,1,0:T(4,128)S(1)}, f32[2,9,4,188]{3,2,1,0:T(4,128)S(1)}, f32[2,9,4,188]{3,2,1,0:T(4,128)S(1)}) custom-call(s32[2,2]{1,0:T(2,128)S(1)} %bitcast.9, s32[2,2]{1,0:T(2,128)S(1)} %bitcast.11, s32[2,2]{1,0:T(2,128)S(1)} %bitcast.10, s32[2,128]{1,0:T(2,128)S(1)} %copy-done.3, f32[64,188]{1,0:T(8,128)S(1)} %copy-done.1, ...), custom_call_target="tpu_custom_call" | custom-call | tf_op jit(solution)/shard_map/nulls/pallas_call | solution.py:390
  16.7 1.5 %collective-permute-start.2 = (f32[2,9,4,188]{3,2,1,0:T(4,128)S(1)}, f32[2,9,4,188]{3,2,1,0:T(4,128)S(1)}, u32[]{:S(2)}, u32[]{:S(2)}) collective-permute-start(f32[2,9,4,188]{3,2,1,0:T(4,128)S(1)} %get-tuple-element.15), channel_id=1, source_target_pairs={{0,4},{1,5},{2,6},{3,7},{4,0},{5,1},{6,2},{7,3},{8,12},{9,13},{10,... | collective-permute-start | bytes 162440 | tf_op jit(solution)/shard_map/ppermute | solution.py:356
  18.1 0.0 collective-permute-start.3
  18.1 1.8 %collective-permute-done.2.a_ref = f32[2,9,4,188]{3,2,1,0:T(4,128)S(1)} collective-permute-done((f32[2,9,4,188]{3,2,1,0:T(4,128)S(1)}, f32[2,9,4,188]{3,2,1,0:T(4,128)S(1)}, u32[]{:S(2)}, u32[]{:S(2)}) %collective-permute-start.2) | collective-permute-done | bytes 54176 | tf_op jit(solution)/shard_map/ppermute | solution.py:356
  19.9 2.3 %collective-permute-done.3.b_ref = f32[2,9,4,188]{3,2,1,0:T(4,128)S(1)} collective-permute-done((f32[2,9,4,188]{3,2,1,0:T(4,128)S(1)}, f32[2,9,4,188]{3,2,1,0:T(4,128)S(1)}, u32[]{:S(2)}, u32[]{:S(2)}) %collective-permute-start.3) | collective-permute-done | bytes 54176 | tf_op jit(solution)/shard_map/ppermute | solution.py:356
  22.3 0.0 collective-permute-done.4.refs_0_.refs_3_
  22.3 2.5 %next_beams.1 = (bf16[3,324,128]{2,1,0:T(8,128)(2,1)S(1)}, bf16[324,128]{1,0:T(8,128)(2,1)S(1)}, bf16[324,128]{1,0:T(8,128)(2,1)S(1)}, bf16[324,128]{1,0:T(8,128)(2,1)S(1)}, bf16[9,160,188]{2,1,0:T(8,128)(2,1)S(1)}) custom-call(bf16[2,2,9,376,128]{4,3,2,1,0:T(8,128)(2,1)S(1)} %bitcast.8, bf16[2,9,2,36,188]{4,3,2,1,0:T(8,128)(2,1)S(1)} %copy.7.w_ref, ...), custom_call_target="tpu_custom_call" | custom-call | tf_op jit(solution)/shard_map/next_beams/pallas_call | solution.py:406
  24.8 3.5 %collective-permute-start.5 = (bf16[3,324,128]{2,1,0:T(8,128)(2,1)S(1)}, bf16[3,324,128]{2,1,0:T(8,128)(2,1)S(1)}, u32[]{:S(2)}, u32[]{:S(2)}) collective-permute-start(bf16[3,324,128]{2,1,0:T(8,128)(2,1)S(1)} %get-tuple-element.20), channel_id=1, source_target_pairs={{0,1},{1,0},{2,3},{3,2},{4,5},{5,4},{6,7},{7,6},{8,9},{9,8},{10,11... | collective-permute-start | bytes 746504 | tf_op jit(solution)/shard_map/ppermute | solution.py:362
  28.3 0.2 collective-permute-start.6
  28.5 1.5 %collective-permute-start.7 = (bf16[324,128]{1,0:T(8,128)(2,1)S(1)}, bf16[324,128]{1,0:T(8,128)(2,1)S(1)}, u32[]{:S(2)}, u32[]{:S(2)}) collective-permute-start(bf16[324,128]{1,0:T(8,128)(2,1)S(1)} %get-tuple-element.22), channel_id=1, source_target_pairs={{0,3},{1,2},{2,1},{3,0},{4,7},{5,6},{6,5},{7,4},{8,11},{9,10},{10,... | collective-permute-start | bytes 248840 | tf_op jit(solution)/shard_map/ppermute | solution.py:362
  30.0 1.5 %last_nulls.1 = bf16[2,9,2,36,188]{4,3,2,1,0:T(8,128)(2,1)S(1)} custom-call(bf16[9,160,188]{2,1,0:T(8,128)(2,1)S(1)} %get-tuple-element.23.w_ref, f32[2,9,4,188]{3,2,1,0:T(4,128)S(1)} %get-tuple-element.14.own_ref, f32[2,9,4,188]{3,2,1,0:T(4,128)S(1)} %collective-permute-done.2.a_ref, f32[2,9,4,188]{3,2,1,0:T(4,128)S(1)} %collective-permute-done.3.b_ref), custom_call_target="tpu_custom_call" | custom-call | tf_op jit(solution)/shard_map/last_nulls/pallas_call | solution.py:418
  31.5 1.4 %copy.9 = bf16[2,9,2,36,188]{4,2,3,1,0:T(2,128)(2,1)} copy(bf16[2,9,2,36,188]{4,3,2,1,0:T(8,128)(2,1)S(1)} %last_nulls.1) | data formatting | bytes 974592
  32.9 0.0 collective-permute-done.6.refs_4_
  32.9 1.4 %collective-permute-done.7.refs_5_ = bf16[324,128]{1,0:T(8,128)(2,1)S(1)} collective-permute-done((bf16[324,128]{1,0:T(8,128)(2,1)S(1)}, bf16[324,128]{1,0:T(8,128)(2,1)S(1)}, u32[]{:S(2)}, u32[]{:S(2)}) %collective-permute-start.7) | collective-permute-done | bytes 82976 | tf_op jit(solution)/shard_map/ppermute | solution.py:362
  34.3 0.0 collective-permute-done.5.refs_2_
  34.3 1.6 %correlate.1 = f32[2,9,2,1296]{3,2,1,0:T(2,128)} custom-call(bf16[324,128]{1,0:T(8,128)(2,1)S(1)} %get-tuple-element.13.refs_0_, bf16[324,128]{1,0:T(8,128)(2,1)S(1)} %get-tuple-element.19.refs_1_, bf16[3,324,128]{2,1,0:T(8,128)(2,1)S(1)} %collective-permute-done.5.refs_2_, bf16[2,324,128]{2,1,0:T(8,128)(2,1)S(1)} %collective-permute-done.4.refs_0_.refs_3_, ...), custom_call_target="tpu_custom_call" | custom-call | tf_op jit(solution)/shard_map/correlate/pallas_call | solution.py:430
Async XLA Ops:
  0.6 11.1 %copy-start = (bf16[2,2,9,2,188,128]{5,3,4,2,1,0:T(2,128)(2,1)S(1)}, bf16[2,2,9,2,188,128]{5,3,4,2,1,0:T(2,128)(2,1)}, u32[]{:S(2)}) copy-start(bf16[2,2,9,2,188,128]{5,3,4,2,1,0:T(2,128)(2,1)} %param.5) | copy-start | bytes 10395652
  0.6 7.2 %copy-start.2 = (s32[2,1,2]{2,1,0:T(1,128)S(1)}, s32[2,1,2]{2,1,0:T(1,128)}, u32[]{:S(2)}) copy-start(s32[2,1,2]{2,1,0:T(1,128)} %param.7) | copy-start | bytes 52
  0.7 11.0 %copy-start.1 = (f32[64,188]{1,0:T(8,128)S(1)}, f32[64,188]{1,0:T(8,128)}, u32[]{:S(2)}) copy-start(f32[64,188]{1,0:T(8,128)} %ang_ref.1) | copy-start | bytes 144388
  0.7 11.0 %copy-start.3 = (s32[2,128]{1,0:T(2,128)S(1)}, s32[2,128]{1,0:T(2,128)}, u32[]{:S(2)}) copy-start(s32[2,128]{1,0:T(2,128)} %off_ref.1) | copy-start | bytes 3076
  6.6 15.7 %collective-permute-start.4 = (bf16[2,324,128]{2,1,0:T(8,128)(2,1)S(1)}, bf16[2,324,128]{2,1,0:T(8,128)(2,1)S(1)}, u32[]{:S(2)}, u32[]{:S(2)}) collective-permute-start(bf16[2,324,128]{2,1,0:T(8,128)(2,1)S(1)} %get-tuple-element.18), channel_id=1, source_target_pairs={{0,2},{1,3},{2,0},{3,1},{4,6},{5,7},{6,4},{7,5},{8,10},{9,11},{10,... | collective-permute-start | bytes 497672 | tf_op jit(solution)/shard_map/ppermute | solution.py:362
  7.9 3.3 %collective-permute-start.1 = (s32[2,1,2]{2,1,0:T(1,128)S(1)}, s32[2,1,2]{2,1,0:T(1,128)S(1)}, u32[]{:S(2)}, u32[]{:S(2)}) collective-permute-start(s32[2,1,2]{2,1,0:T(1,128)S(1)} %copy-done.2), channel_id=1, source_target_pairs={{0,1},{1,0},{2,3},{3,2},{4,8},{5,9},{6,10},{7,11},{8,4},{9,5},{10,... | collective-permute-start | bytes 56 | tf_op jit(solution)/shard_map/ppermute | solution.py:356
  9.0 2.7 %collective-permute-start = (s32[2,1,2]{2,1,0:T(1,128)S(1)}, s32[2,1,2]{2,1,0:T(1,128)S(1)}, u32[]{:S(2)}, u32[]{:S(2)}) collective-permute-start(s32[2,1,2]{2,1,0:T(1,128)S(1)} %copy-done.2), channel_id=1, source_target_pairs={{0,4},{1,5},{2,6},{3,7},{4,0},{5,1},{6,2},{7,3},{8,12},{9,13},{10,... | collective-permute-start | bytes 56 | tf_op jit(solution)/shard_map/ppermute | solution.py:356
  16.7 3.3 %collective-permute-start.2 = (f32[2,9,4,188]{3,2,1,0:T(4,128)S(1)}, f32[2,9,4,188]{3,2,1,0:T(4,128)S(1)}, u32[]{:S(2)}, u32[]{:S(2)}) collective-permute-start(f32[2,9,4,188]{3,2,1,0:T(4,128)S(1)} %get-tuple-element.15), channel_id=1, source_target_pairs={{0,4},{1,5},{2,6},{3,7},{4,0},{5,1},{6,2},{7,3},{8,12},{9,13},{10,... | collective-permute-start | bytes 162440 | tf_op jit(solution)/shard_map/ppermute | solution.py:356
  18.1 4.2 %collective-permute-start.3 = (f32[2,9,4,188]{3,2,1,0:T(4,128)S(1)}, f32[2,9,4,188]{3,2,1,0:T(4,128)S(1)}, u32[]{:S(2)}, u32[]{:S(2)}) collective-permute-start(f32[2,9,4,188]{3,2,1,0:T(4,128)S(1)} %get-tuple-element.16), channel_id=1, source_target_pairs={{0,1},{1,0},{2,3},{3,2},{4,8},{5,9},{6,10},{7,11},{8,4},{9,5},{10,... | collective-permute-start | bytes 162440 | tf_op jit(solution)/shard_map/ppermute | solution.py:356
  24.8 9.5 %collective-permute-start.5 = (bf16[3,324,128]{2,1,0:T(8,128)(2,1)S(1)}, bf16[3,324,128]{2,1,0:T(8,128)(2,1)S(1)}, u32[]{:S(2)}, u32[]{:S(2)}) collective-permute-start(bf16[3,324,128]{2,1,0:T(8,128)(2,1)S(1)} %get-tuple-element.20), channel_id=1, source_target_pairs={{0,1},{1,0},{2,3},{3,2},{4,5},{5,4},{6,7},{7,6},{8,9},{9,8},{10,11... | collective-permute-start | bytes 746504 | tf_op jit(solution)/shard_map/ppermute | solution.py:362
  28.3 4.6 %collective-permute-start.6 = (bf16[324,128]{1,0:T(8,128)(2,1)S(1)}, bf16[324,128]{1,0:T(8,128)(2,1)S(1)}, u32[]{:S(2)}, u32[]{:S(2)}) collective-permute-start(bf16[324,128]{1,0:T(8,128)(2,1)S(1)} %get-tuple-element.21), channel_id=1, source_target_pairs={{0,2},{1,3},{2,0},{3,1},{4,6},{5,7},{6,4},{7,5},{8,10},{9,11},{10,... | collective-permute-start | bytes 248840 | tf_op jit(solution)/shard_map/ppermute | solution.py:362
  28.5 5.8 %collective-permute-start.7 = (bf16[324,128]{1,0:T(8,128)(2,1)S(1)}, bf16[324,128]{1,0:T(8,128)(2,1)S(1)}, u32[]{:S(2)}, u32[]{:S(2)}) collective-permute-start(bf16[324,128]{1,0:T(8,128)(2,1)S(1)} %get-tuple-element.22), channel_id=1, source_target_pairs={{0,3},{1,2},{2,1},{3,0},{4,7},{5,6},{6,5},{7,4},{8,11},{9,10},{10,... | collective-permute-start | bytes 248840 | tf_op jit(solution)/shard_map/ppermute | solution.py:362

commit v3 on v2

--- a/solution.py
+++ b/solution.py
@@ -45,12 +45,17 @@
     return lax.dot_general(left, right, (((1,), (1,)), ((), ())), preferred_element_type=F32)
 
 
-def beams_of(weight_rows, spread, keep, x_real, x_imag):
+def spread_rows(weight_rows, spread, keep):
     wide = jnp.where(keep, dot(weight_rows, spread), 0.0)
     half = wide.shape[0] // 2
     real, imag = wide[:half], wide[half:]
     on_real = jnp.concatenate([real, -imag]).astype(BF16)
     on_imag = jnp.concatenate([imag, real]).astype(BF16)
+    return on_real, on_imag
+
+
+def beams_of(weight_rows, spread, keep, x_real, x_imag):
+    on_real, on_imag = spread_rows(weight_rows, spread, keep)
     return dot(on_real, x_real) + dot(on_imag, x_imag)
 
 
@@ -91,21 +96,21 @@
     return jnp.concatenate(pieces)
 
 
-def first_beams_kernel(dims, x_ref, w_ref, *refs):
-    (near, mine, *far), (stage, held, sems) = refs[:-3], refs[-3:]
-    dishes = x_ref.shape[2]
+def spread_kernel(dims, w_ref, out_ref):
     chans, pad_beams = dims[1], dims[4]
-    copies = []
-    for d in range(dishes):
-        copies.append(pltpu.make_async_copy(x_ref.at[0, :, d], held.at[:, d], sems.at[d]))
-        copies[d].start()
     ports = w_ref.shape[-1]
     spread = spread_matrix(ports, chans)
     keep = own_channel(2 * chans * pad_beams, pad_beams, ports, chans)
-    for d in range(dishes):
+    for d in range(w_ref.shape[1]):
         rows = weight_rows_of(w_ref, d, pad_beams).astype(BF16)
-        copies[d].wait()
-        put_beams(beams_of(rows, spread, keep, held[0, d], held[1, d]), stage, d, dims)
+        out_ref[d, 0], out_ref[d, 1] = spread_rows(rows, spread, keep)
+
+
+def first_beams_kernel(dims, x_ref, wide_ref, *refs):
+    (near, mine, *far), stage = refs[:-1], refs[-1]
+    for d in range(x_ref.shape[2]):
+        rows = dot(wide_ref[d, 0], x_ref[0, 0, d]) + dot(wide_ref[d, 1], x_ref[0, 1, d])
+        put_beams(rows, stage, d, dims)
     flush_beams(stage, [mine, near], [0, 1], dims)
     for i, out in enumerate(far):
         flush_beams(stage, [out.at[0], out.at[1]], [2 * i + 2, 2 * i + 3], dims)
@@ -370,19 +375,23 @@
     several = jax.ShapeDtypeStruct((groups // 2 + 1, chunk, samples), BF16)
     stage = pltpu.VMEM((groups * stage_rows(dims), samples), F32)
 
+    wide_rows = pl.pallas_call(
+        functools.partial(spread_kernel, dims),
+        out_shape=jax.ShapeDtypeStruct((dishes, 2, 2 * chans * pad_beams, wide), BF16),
+        in_specs=[vmem()],
+        out_specs=vmem(),
+        compiler_params=params(),
+        name="spread",
+    )(weights)
     first_near, first_mine, *first_far = pl.pallas_call(
         functools.partial(first_beams_kernel, dims),
         out_shape=(piece, piece) + (two,) * (groups // 2 - 1),
-        in_specs=[pl.BlockSpec(memory_space=pltpu.HBM), vmem()],
+        in_specs=[vmem()] * 2,
         out_specs=(vmem(),) * (groups // 2 + 1),
-        scratch_shapes=[
-            stage,
-            pltpu.VMEM((2, dishes, wide, samples), BF16),
-            pltpu.SemaphoreType.DMA((dishes,)),
-        ],
+        scratch_shapes=[stage],
         compiler_params=params(),
         name="first_beams",
-    )(pltpu.with_memory_space_constraint(x, pltpu.HBM), weights)
+    )(x, wide_rows)
     first_got = [step_over(value, 2 * i + 2) for i, value in enumerate(first_far)]
 
     rows = chans * 2 * slots

time: 36.1 us -> 33 us (0.914)
  the two profiles are of different devices: /device:TPU:9 before, /device:TPU:17 now
where the time goes in v3:
time: 33 us; the launch traced here: 32.9 us
  Pallas kernels  12 us (36%)
  starting transfers between devices  9.66 us (29%)
  waiting for transfers between devices  7.64 us (23%)
  local copies, waits for them, and re-layouts  2.86 us (9%)
  between operations  0.71 us (2%)
    ppermute x4, starting transfers between devices, step_over(): lax.ppermute(value, 'section', [(i, i ^ step) for i in range(groups)])  6.89 us
    ppermute x4, waiting for transfers between devices, swap(): return lax.ppermute(value, ('chan', 'section'), path)  6.19 us
    pallas_call x1, Pallas kernels, per_device(): pl.pallas_call(nulls_kernel, out_shape=(vectors,) * 3, in_specs=[smem(),...  4.97 us
    unnamed x10, local copies, waits for them, and re-layouts  2.86 us
    ppermute x4, starting transfers between devices, swap(): return lax.ppermute(value, ('chan', 'section'), path)  2.77 us
    pallas_call x1, Pallas kernels, per_device(): pl.pallas_call(functools.partial(next_beams_kernel, dims, 0), out_shape=(...  2.48 us
    pallas_call x1, Pallas kernels, per_device(): pl.pallas_call(functools.partial(correlate_kernel, dims, 1.0 / (cycles *...  1.62 us
    pallas_call x1, Pallas kernels, per_device(): pl.pallas_call(functools.partial(last_nulls_kernel, dims, 1), out_shape=j...  1.5 us
  transfers between devices with their start and end apart: 8, of which 5 were waited for; matrix products, arithmetic and copies ran while one was open for 4% of the time, Pallas kernels for 20%

profile of v3, /device:TPU:17, one launch (start us, length us, event | category | flops | bytes accessed | tf_op | source)
XLA Modules:
  0.0 32.9 jit_solution(85740745579969247)
XLA Ops:
  0.6 0.0 copy-start
  0.6 1.3 %copy.7.w_ref = bf16[2,9,2,36,188]{4,3,2,1,0:T(8,128)(2,1)S(1)} copy(bf16[2,9,2,36,188]{4,2,3,1,0:T(2,128)(2,1)} %param.6) | data formatting | bytes 974592 | tf_op args[1]
  2.0 0.6 %spread.1.wide_ref = bf16[9,2,160,376]{3,2,1,0:T(8,128)(2,1)S(1)} custom-call(bf16[2,9,2,36,188]{4,3,2,1,0:T(8,128)(2,1)S(1)} %copy.7.w_ref), custom_call_target="tpu_custom_call" | custom-call | tf_op jit(solution)/shard_map/spread/pallas_call | solution.py:378
  2.6 0.0 copy-start.2
  2.6 0.0 copy-start.1
  2.7 0.0 copy-start.3
  2.7 0.1 copy-done
  2.8 0.8 %first_beams.1 = (bf16[324,128]{1,0:T(8,128)(2,1)S(1)}, bf16[324,128]{1,0:T(8,128)(2,1)S(1)}, bf16[2,324,128]{2,1,0:T(8,128)(2,1)S(1)}) custom-call(bf16[2,2,9,376,128]{4,3,2,1,0:T(8,128)(2,1)S(1)} %bitcast.6, bf16[9,2,160,376]{3,2,1,0:T(8,128)(2,1)S(1)} %spread.1.wide_ref), custom_call_target="tpu_custom_call" | custom-call | tf_op jit(solution)/shard_map/first_beams/pallas_call | solution.py:386
  3.6 1.3 %collective-permute-start.4 = (bf16[2,324,128]{2,1,0:T(8,128)(2,1)S(1)}, bf16[2,324,128]{2,1,0:T(8,128)(2,1)S(1)}, u32[]{:S(2)}, u32[]{:S(2)}) collective-permute-start(bf16[2,324,128]{2,1,0:T(8,128)(2,1)S(1)} %get-tuple-element.18), channel_id=1, source_target_pairs={{0,2},{1,3},{2,0},{3,1},{4,6},{5,7},{6,4},{7,5},{8,10},{9,11},{10,... | collective-permute-start | bytes 497672 | tf_op jit(solution)/shard_map/ppermute | solution.py:367
  4.9 0.0 copy-done.2
  4.9 1.2 %collective-permute-start = (s32[2,1,2]{2,1,0:T(1,128)S(1)}, s32[2,1,2]{2,1,0:T(1,128)S(1)}, u32[]{:S(2)}, u32[]{:S(2)}) collective-permute-start(s32[2,1,2]{2,1,0:T(1,128)S(1)} %copy-done.2), channel_id=1, source_target_pairs={{0,4},{1,5},{2,6},{3,7},{4,0},{5,1},{6,2},{7,3},{8,12},{9,13},{10,... | collective-permute-start | bytes 56 | tf_op jit(solution)/shard_map/ppermute | solution.py:361
  6.1 0.1 collective-permute-start.1
  6.3 1.4 %collective-permute-done = s32[2,1,2]{2,1,0:T(1,128)S(1)} collective-permute-done((s32[2,1,2]{2,1,0:T(1,128)S(1)}, s32[2,1,2]{2,1,0:T(1,128)S(1)}, u32[]{:S(2)}, u32[]{:S(2)}) %collective-permute-start) | collective-permute-done | bytes 48 | tf_op jit(solution)/shard_map/ppermute | solution.py:361
  7.7 1.8 %collective-permute-done.1 = s32[2,1,2]{2,1,0:T(1,128)S(1)} collective-permute-done((s32[2,1,2]{2,1,0:T(1,128)S(1)}, s32[2,1,2]{2,1,0:T(1,128)S(1)}, u32[]{:S(2)}, u32[]{:S(2)}) %collective-permute-start.1) | collective-permute-done | bytes 48 | tf_op jit(solution)/shard_map/ppermute | solution.py:361
  9.5 0.0 copy-done.1
  9.5 0.0 copy-done.3
  9.5 5.0 %nulls.1 = (f32[2,9,4,188]{3,2,1,0:T(4,128)S(1)}, f32[2,9,4,188]{3,2,1,0:T(4,128)S(1)}, f32[2,9,4,188]{3,2,1,0:T(4,128)S(1)}) custom-call(s32[2,2]{1,0:T(2,128)S(1)} %bitcast.9, s32[2,2]{1,0:T(2,128)S(1)} %bitcast.10, s32[2,2]{1,0:T(2,128)S(1)} %bitcast.11, s32[2,128]{1,0:T(2,128)S(1)} %copy-done.3, f32[64,188]{1,0:T(8,128)S(1)} %copy-done.1, ...), custom_call_target="tpu_custom_call" | custom-call | tf_op jit(solution)/shard_map/nulls/pallas_call | solution.py:399
  14.4 0.3 collective-permute-start.2
  14.8 1.1 %collective-permute-start.3 = (f32[2,9,4,188]{3,2,1,0:T(4,128)S(1)}, f32[2,9,4,188]{3,2,1,0:T(4,128)S(1)}, u32[]{:S(2)}, u32[]{:S(2)}) collective-permute-start(f32[2,9,4,188]{3,2,1,0:T(4,128)S(1)} %get-tuple-element.16), channel_id=1, source_target_pairs={{0,1},{1,0},{2,3},{3,2},{4,8},{5,9},{6,10},{7,11},{8,4},{9,5},{10,... | collective-permute-start | bytes 162440 | tf_op jit(solution)/shard_map/ppermute | solution.py:361
  15.9 1.9 %collective-permute-done.2.a_ref = f32[2,9,4,188]{3,2,1,0:T(4,128)S(1)} collective-permute-done((f32[2,9,4,188]{3,2,1,0:T(4,128)S(1)}, f32[2,9,4,188]{3,2,1,0:T(4,128)S(1)}, u32[]{:S(2)}, u32[]{:S(2)}) %collective-permute-start.2) | collective-permute-done | bytes 54176 | tf_op jit(solution)/shard_map/ppermute | solution.py:361
  17.7 1.2 %collective-permute-done.3.b_ref = f32[2,9,4,188]{3,2,1,0:T(4,128)S(1)} collective-permute-done((f32[2,9,4,188]{3,2,1,0:T(4,128)S(1)}, f32[2,9,4,188]{3,2,1,0:T(4,128)S(1)}, u32[]{:S(2)}, u32[]{:S(2)}) %collective-permute-start.3) | collective-permute-done | bytes 54176 | tf_op jit(solution)/shard_map/ppermute | solution.py:361
  18.9 0.0 collective-permute-done.4.refs_0_.refs_3_
  18.9 2.5 %next_beams.1 = (bf16[3,324,128]{2,1,0:T(8,128)(2,1)S(1)}, bf16[324,128]{1,0:T(8,128)(2,1)S(1)}, bf16[324,128]{1,0:T(8,128)(2,1)S(1)}, bf16[324,128]{1,0:T(8,128)(2,1)S(1)}, bf16[9,160,188]{2,1,0:T(8,128)(2,1)S(1)}) custom-call(bf16[2,2,9,376,128]{4,3,2,1,0:T(8,128)(2,1)S(1)} %bitcast.8, bf16[2,9,2,36,188]{4,3,2,1,0:T(8,128)(2,1)S(1)} %copy.7.w_ref, ...), custom_call_target="tpu_custom_call" | custom-call | tf_op jit(solution)/shard_map/next_beams/pallas_call | solution.py:415
  21.4 3.9 %collective-permute-start.5 = (bf16[3,324,128]{2,1,0:T(8,128)(2,1)S(1)}, bf16[3,324,128]{2,1,0:T(8,128)(2,1)S(1)}, u32[]{:S(2)}, u32[]{:S(2)}) collective-permute-start(bf16[3,324,128]{2,1,0:T(8,128)(2,1)S(1)} %get-tuple-element.20), channel_id=1, source_target_pairs={{0,1},{1,0},{2,3},{3,2},{4,5},{5,4},{6,7},{7,6},{8,9},{9,8},{10,11... | collective-permute-start | bytes 746504 | tf_op jit(solution)/shard_map/ppermute | solution.py:367
  25.2 0.2 collective-permute-start.6
  25.5 1.5 %collective-permute-start.7 = (bf16[324,128]{1,0:T(8,128)(2,1)S(1)}, bf16[324,128]{1,0:T(8,128)(2,1)S(1)}, u32[]{:S(2)}, u32[]{:S(2)}) collective-permute-start(bf16[324,128]{1,0:T(8,128)(2,1)S(1)} %get-tuple-element.22), channel_id=1, source_target_pairs={{0,3},{1,2},{2,1},{3,0},{4,7},{5,6},{6,5},{7,4},{8,11},{9,10},{10,... | collective-permute-start | bytes 248840 | tf_op jit(solution)/shard_map/ppermute | solution.py:367
  26.9 1.5 %last_nulls.1 = bf16[2,9,2,36,188]{4,3,2,1,0:T(8,128)(2,1)S(1)} custom-call(bf16[9,160,188]{2,1,0:T(8,128)(2,1)S(1)} %get-tuple-element.23.w_ref, f32[2,9,4,188]{3,2,1,0:T(4,128)S(1)} %get-tuple-element.14.own_ref, f32[2,9,4,188]{3,2,1,0:T(4,128)S(1)} %collective-permute-done.2.a_ref, f32[2,9,4,188]{3,2,1,0:T(4,128)S(1)} %collective-permute-done.3.b_ref), custom_call_target="tpu_custom_call" | custom-call | tf_op jit(solution)/shard_map/last_nulls/pallas_call | solution.py:427
  28.5 1.4 %copy.9 = bf16[2,9,2,36,188]{4,2,3,1,0:T(2,128)(2,1)} copy(bf16[2,9,2,36,188]{4,3,2,1,0:T(8,128)(2,1)S(1)} %last_nulls.1) | data formatting | bytes 974592
  29.8 0.0 collective-permute-done.6.refs_4_
  29.8 1.4 %collective-permute-done.7.refs_5_ = bf16[324,128]{1,0:T(8,128)(2,1)S(1)} collective-permute-done((bf16[324,128]{1,0:T(8,128)(2,1)S(1)}, bf16[324,128]{1,0:T(8,128)(2,1)S(1)}, u32[]{:S(2)}, u32[]{:S(2)}) %collective-permute-start.7) | collective-permute-done | bytes 82976 | tf_op jit(solution)/shard_map/ppermute | solution.py:367
  31.3 0.0 collective-permute-done.5.refs_2_
  31.3 1.6 %correlate.1 = f32[2,9,2,1296]{3,2,1,0:T(2,128)} custom-call(bf16[324,128]{1,0:T(8,128)(2,1)S(1)} %get-tuple-element.13.refs_0_, bf16[324,128]{1,0:T(8,128)(2,1)S(1)} %get-tuple-element.19.refs_1_, bf16[3,324,128]{2,1,0:T(8,128)(2,1)S(1)} %collective-permute-done.5.refs_2_, bf16[2,324,128]{2,1,0:T(8,128)(2,1)S(1)} %collective-permute-done.4.refs_0_.refs_3_, ...), custom_call_target="tpu_custom_call" | custom-call | tf_op jit(solution)/shard_map/correlate/pallas_call | solution.py:439
Async XLA Ops:
  0.6 2.2 %copy-start = (bf16[2,2,9,2,188,128]{5,3,4,2,1,0:T(2,128)(2,1)S(1)}, bf16[2,2,9,2,188,128]{5,3,4,2,1,0:T(2,128)(2,1)}, u32[]{:S(2)}) copy-start(bf16[2,2,9,2,188,128]{5,3,4,2,1,0:T(2,128)(2,1)} %param.5) | copy-start | bytes 10395652
  2.6 2.3 %copy-start.2 = (s32[2,1,2]{2,1,0:T(1,128)S(1)}, s32[2,1,2]{2,1,0:T(1,128)}, u32[]{:S(2)}) copy-start(s32[2,1,2]{2,1,0:T(1,128)} %param.7) | copy-start | bytes 52
  2.6 6.8 %copy-start.1 = (f32[64,188]{1,0:T(8,128)S(1)}, f32[64,188]{1,0:T(8,128)}, u32[]{:S(2)}) copy-start(f32[64,188]{1,0:T(8,128)} %ang_ref.1) | copy-start | bytes 144388
  2.7 6.8 %copy-start.3 = (s32[2,128]{1,0:T(2,128)S(1)}, s32[2,128]{1,0:T(2,128)}, u32[]{:S(2)}) copy-start(s32[2,128]{1,0:T(2,128)} %off_ref.1) | copy-start | bytes 3076
  3.6 15.3 %collective-permute-start.4 = (bf16[2,324,128]{2,1,0:T(8,128)(2,1)S(1)}, bf16[2,324,128]{2,1,0:T(8,128)(2,1)S(1)}, u32[]{:S(2)}, u32[]{:S(2)}) collective-permute-start(bf16[2,324,128]{2,1,0:T(8,128)(2,1)S(1)} %get-tuple-element.18), channel_id=1, source_target_pairs={{0,2},{1,3},{2,0},{3,1},{4,6},{5,7},{6,4},{7,5},{8,10},{9,11},{10,... | collective-permute-start | bytes 497672 | tf_op jit(solution)/shard_map/ppermute | solution.py:367
  4.9 2.7 %collective-permute-start = (s32[2,1,2]{2,1,0:T(1,128)S(1)}, s32[2,1,2]{2,1,0:T(1,128)S(1)}, u32[]{:S(2)}, u32[]{:S(2)}) collective-permute-start(s32[2,1,2]{2,1,0:T(1,128)S(1)} %copy-done.2), channel_id=1, source_target_pairs={{0,4},{1,5},{2,6},{3,7},{4,0},{5,1},{6,2},{7,3},{8,12},{9,13},{10,... | collective-permute-start | bytes 56 | tf_op jit(solution)/shard_map/ppermute | solution.py:361
  6.1 3.3 %collective-permute-start.1 = (s32[2,1,2]{2,1,0:T(1,128)S(1)}, s32[2,1,2]{2,1,0:T(1,128)S(1)}, u32[]{:S(2)}, u32[]{:S(2)}) collective-permute-start(s32[2,1,2]{2,1,0:T(1,128)S(1)} %copy-done.2), channel_id=1, source_target_pairs={{0,1},{1,0},{2,3},{3,2},{4,8},{5,9},{6,10},{7,11},{8,4},{9,5},{10,... | collective-permute-start | bytes 56 | tf_op jit(solution)/shard_map/ppermute | solution.py:361
  14.4 3.3 %collective-permute-start.2 = (f32[2,9,4,188]{3,2,1,0:T(4,128)S(1)}, f32[2,9,4,188]{3,2,1,0:T(4,128)S(1)}, u32[]{:S(2)}, u32[]{:S(2)}) collective-permute-start(f32[2,9,4,188]{3,2,1,0:T(4,128)S(1)} %get-tuple-element.15), channel_id=1, source_target_pairs={{0,4},{1,5},{2,6},{3,7},{4,0},{5,1},{6,2},{7,3},{8,12},{9,13},{10,... | collective-permute-start | bytes 162440 | tf_op jit(solution)/shard_map/ppermute | solution.py:361
  14.8 4.1 %collective-permute-start.3 = (f32[2,9,4,188]{3,2,1,0:T(4,128)S(1)}, f32[2,9,4,188]{3,2,1,0:T(4,128)S(1)}, u32[]{:S(2)}, u32[]{:S(2)}) collective-permute-start(f32[2,9,4,188]{3,2,1,0:T(4,128)S(1)} %get-tuple-element.16), channel_id=1, source_target_pairs={{0,1},{1,0},{2,3},{3,2},{4,8},{5,9},{6,10},{7,11},{8,4},{9,5},{10,... | collective-permute-start | bytes 162440 | tf_op jit(solution)/shard_map/ppermute | solution.py:361
  21.4 9.9 %collective-permute-start.5 = (bf16[3,324,128]{2,1,0:T(8,128)(2,1)S(1)}, bf16[3,324,128]{2,1,0:T(8,128)(2,1)S(1)}, u32[]{:S(2)}, u32[]{:S(2)}) collective-permute-start(bf16[3,324,128]{2,1,0:T(8,128)(2,1)S(1)} %get-tuple-element.20), channel_id=1, source_target_pairs={{0,1},{1,0},{2,3},{3,2},{4,5},{5,4},{6,7},{7,6},{8,9},{9,8},{10,11... | collective-permute-start | bytes 746504 | tf_op jit(solution)/shard_map/ppermute | solution.py:367
  25.2 4.6 %collective-permute-start.6 = (bf16[324,128]{1,0:T(8,128)(2,1)S(1)}, bf16[324,128]{1,0:T(8,128)(2,1)S(1)}, u32[]{:S(2)}, u32[]{:S(2)}) collective-permute-start(bf16[324,128]{1,0:T(8,128)(2,1)S(1)} %get-tuple-element.21), channel_id=1, source_target_pairs={{0,2},{1,3},{2,0},{3,1},{4,6},{5,7},{6,4},{7,5},{8,10},{9,11},{10,... | collective-permute-start | bytes 248840 | tf_op jit(solution)/shard_map/ppermute | solution.py:367
  25.5 5.8 %collective-permute-start.7 = (bf16[324,128]{1,0:T(8,128)(2,1)S(1)}, bf16[324,128]{1,0:T(8,128)(2,1)S(1)}, u32[]{:S(2)}, u32[]{:S(2)}) collective-permute-start(bf16[324,128]{1,0:T(8,128)(2,1)S(1)} %get-tuple-element.22), channel_id=1, source_target_pairs={{0,3},{1,2},{2,1},{3,0},{4,7},{5,6},{6,5},{7,4},{8,11},{9,10},{10,... | collective-permute-start | bytes 248840 | tf_op jit(solution)/shard_map/ppermute | solution.py:367

commit v4 on v3

--- a/solution.py
+++ b/solution.py
@@ -120,82 +120,77 @@
     return lax.rem(lax.axis_index("chan"), 2) == 0
 
 
-def nulls_kernel(sat_ref, sat_a_ref, sat_b_ref, off_ref, ang_ref, x_ref,
-                 own_ref, a_ref, b_ref, phase, folded):
-    cycles, _, dishes, wide, samples = x_ref.shape
+def stacked_halves(real, imag):
+    real_h, real_l = split(real)
+    imag_h, imag_l = split(imag)
+    return jnp.concatenate(
+        [real_h.astype(F32), real_l.astype(F32), imag_h.astype(F32), imag_l.astype(F32)]
+    )
+
+
+def nulls_kernel(cycle, sat_ref, sat_a_ref, sat_b_ref, off_ref, ang_ref, x_ref,
+                 own_ref, a_ref, b_ref, phase, inner, folded):
+    _, _, dishes, wide, samples = x_ref.shape
     ports = ang_ref.shape[-1]
     chans = wide // ports
     slots = sat_ref.shape[-1]
     per_chan = 2 * slots
     rows = chans * per_chan
+    half = 2 * rows
     spread = spread_matrix(ports, chans)
     even = even_place()
     place = lax.axis_index("chan")
     last_place = lax.axis_size("chan") - 1
+    for f in range(chans):
+        swapped = even if f == 0 else jnp.logical_not(even)
+        for s in range(slots):
+            base = f * per_chan + s
+            beside = jnp.where(swapped, sat_b_ref[cycle, s], sat_a_ref[cycle, s])
+            phase[pl.ds(base, 1), :] = ang_ref[pl.ds(sat_ref[cycle, s], 1), :]
+            phase[pl.ds(base + slots, 1), :] = ang_ref[pl.ds(beside, 1), :]
+    cosine, sine = jnp.cos(phase[...]), jnp.sin(phase[...])
     time = lax.broadcasted_iota(jnp.int32, (samples, off_ref.shape[1]), 0)
-    ones = jnp.ones((rows, off_ref.shape[1]), BF16)
-    for c in range(cycles):
-        for f in range(chans):
-            swapped = even if f == 0 else jnp.logical_not(even)
-            for s in range(slots):
-                base = f * per_chan + s
-                phase[pl.ds(c * rows + base, 1), :] = ang_ref[pl.ds(sat_ref[c, s], 1), :]
-                phase[pl.ds(c * rows + base + slots, 1), :] = ang_ref[
-                    pl.ds(jnp.where(swapped, sat_b_ref[c, s], sat_a_ref[c, s]), 1), :
-                ]
-    angle = phase[...]
-    cosine, sine = jnp.cos(angle), jnp.sin(angle)
+    hits = jnp.where(time == off_ref[cycle : cycle + 1, :], 1.0, 0.0).astype(BF16)
+    counts = dot_t(jnp.ones((rows, off_ref.shape[1]), BF16), hits)
+    column = stacked_halves(cosine, sine).astype(BF16)
     keep4 = own_channel(4 * rows, per_chan, ports, chans)
+    wide_rows = jnp.where(keep4, dot(column, spread), 0.0)
+    on_real = wide_rows.astype(BF16)
+    on_imag = jnp.concatenate([wide_rows[half:], -wide_rows[:half]]).astype(BF16)
+    for d in range(dishes):
+        inner[d] = dot(on_real, x_ref[cycle, 0, d]) + dot(on_imag, x_ref[cycle, 1, d])
     keep2 = own_channel(2 * rows, per_chan, ports, chans)
-    for c in range(cycles):
-        hits = jnp.where(time == off_ref[c : c + 1, :], 1.0, 0.0).astype(BF16)
-        counts = dot_t(ones, hits)
-        a_real = cosine[c * rows : (c + 1) * rows]
-        a_imag = sine[c * rows : (c + 1) * rows]
-        real_h, real_l = split(a_real)
-        imag_h, imag_l = split(a_imag)
-        column = jnp.concatenate(
-            [real_h.astype(F32), real_l.astype(F32), imag_h.astype(F32), imag_l.astype(F32)]
-        ).astype(BF16)
-        wide_rows = jnp.where(keep4, dot(column, spread), 0.0)
-        half = 2 * rows
-        on_real = wide_rows.astype(BF16)
-        on_imag = jnp.concatenate([wide_rows[half:], -wide_rows[:half]]).astype(BF16)
-        for d in range(dishes):
-            x_real, x_imag = x_ref[c, 0, d], x_ref[c, 1, d]
-            inner = dot(on_real, x_real) + dot(on_imag, x_imag)
-            inner_real = (inner[0:rows] + inner[rows:half]) * counts
-            inner_imag = (inner[half : half + rows] + inner[half + rows :]) * counts
-            real_h, real_l = split(inner_real)
-            imag_h, imag_l = split(inner_imag)
-            pieces = jnp.concatenate(
-                [real_h.astype(F32), real_l.astype(F32), imag_h.astype(F32), imag_l.astype(F32)]
-            )
-            turned = jnp.concatenate([-pieces[half:], pieces[:half]])
-            outer = dot_t(pieces.astype(BF16), x_real) + dot_t(turned.astype(BF16), x_imag)
-            both = jnp.concatenate(
-                [outer[0:rows] + outer[rows:half], outer[half : half + rows] + outer[half + rows :]]
-            )
-            first = (c * dishes + d) * 2 * rows
-            folded[first : first + 2 * rows, :] = jnp.where(keep2, both, 0.0)
+    for d in range(dishes):
+        now = inner[d]
+        pieces = stacked_halves(
+            (now[0:rows] + now[rows:half]) * counts,
+            (now[half : half + rows] + now[half + rows :]) * counts,
+        )
+        turned = jnp.concatenate([-pieces[half:], pieces[:half]])
+        outer = dot_t(pieces.astype(BF16), x_ref[cycle, 0, d]) + dot_t(
+            turned.astype(BF16), x_ref[cycle, 1, d]
+        )
+        both = jnp.concatenate(
+            [outer[0:rows] + outer[rows:half], outer[half : half + rows] + outer[half + rows :]]
+        )
+        folded[d * half : (d + 1) * half, :] = jnp.where(keep2, both, 0.0)
     high, low = split(folded[...])
     summed = dot_t(high, spread) + dot_t(low, spread)
-    for c in range(cycles):
-        for d in range(dishes):
-            first = (c * dishes + d) * 2 * rows
-            for part in range(2):
-                block = summed[first + part * rows : first + (part + 1) * rows]
-                own = block[0:slots]
-                for f in range(1, chans):
-                    own = own + block[f * per_chan : f * per_chan + slots]
-                along = (cosine if part == 0 else sine)[c * rows : c * rows + slots]
-                last = (chans - 1) * per_chan + slots
-                where = slice(part * slots, (part + 1) * slots)
-                own_ref[c, d, where, :] = own + LOADING * along
-                to_dn = jnp.where(place > 0, block[slots : 2 * slots], 0.0)
-                to_up = jnp.where(place < last_place, block[last : last + slots], 0.0)
-                a_ref[c, d, where, :] = jnp.where(even, to_up, to_dn)
-                b_ref[c, d, where, :] = jnp.where(even, to_dn, to_up)
+    for d in range(dishes):
+        for part in range(2):
+            first = (2 * d + part) * rows
+            block = summed[first : first + rows]
+            own = block[0:slots]
+            for f in range(1, chans):
+                own = own + block[f * per_chan : f * per_chan + slots]
+            along = (cosine if part == 0 else sine)[0:slots]
+            last = (chans - 1) * per_chan + slots
+            where = slice(part * slots, (part + 1) * slots)
+            own_ref[d, where, :] = own + LOADING * along
+            to_dn = jnp.where(place > 0, block[slots : 2 * slots], 0.0)
+            to_up = jnp.where(place < last_place, block[last : last + slots], 0.0)
+            a_ref[d, where, :] = jnp.where(even, to_up, to_dn)
+            b_ref[d, where, :] = jnp.where(even, to_dn, to_up)
 
 
 def null_rows(rows, own, beside, chans, pad_beams):
@@ -219,9 +214,9 @@
     return jnp.concatenate(reals + imags)
 
 
-def beside_of(a_ref, b_ref, cycle, d):
+def beside_of(a_ref, b_ref, d):
     even = even_place()
-    a, b = a_ref[cycle, d], b_ref[cycle, d]
+    a, b = a_ref[d], b_ref[d]
     return jnp.where(even, b, a), jnp.where(even, a, b)
 
 
@@ -239,8 +234,8 @@
     for d in range(dishes):
         rows = null_rows(
             weight_rows_of(w_ref, d, pad_beams),
-            own_ref[cycle, d],
-            beside_of(a_ref, b_ref, cycle, d),
+            own_ref[d],
+            beside_of(a_ref, b_ref, d),
             chans,
             pad_beams,
         ).astype(BF16)
@@ -254,14 +249,14 @@
     flush_beams(stage, [mine, near.at[groups // 2], *far], range(groups), dims)
 
 
-def last_nulls_kernel(dims, cycle, w_ref, own_ref, a_ref, b_ref, out_ref):
+def last_nulls_kernel(dims, w_ref, own_ref, a_ref, b_ref, out_ref):
     chans, pad_beams = dims[1], dims[4]
     beams = out_ref.shape[3]
     for d in range(w_ref.shape[0]):
         rows = null_rows(
             w_ref[d].astype(F32),
-            own_ref[cycle, d],
-            beside_of(a_ref, b_ref, cycle, d),
+            own_ref[d],
+            beside_of(a_ref, b_ref, d),
             chans,
             pad_beams,
         )
@@ -395,21 +390,24 @@
     first_got = [step_over(value, 2 * i + 2) for i, value in enumerate(first_far)]
 
     rows = chans * 2 * slots
-    vectors = jax.ShapeDtypeStruct((cycles, dishes, 2 * slots, ports), F32)
-    own, to_a, to_b = pl.pallas_call(
-        nulls_kernel,
-        out_shape=(vectors,) * 3,
-        in_specs=[smem(), smem(), smem(), vmem(), vmem(), vmem()],
-        out_specs=(vmem(),) * 3,
-        scratch_shapes=[
-            pltpu.VMEM((cycles * rows, ports), F32),
-            pltpu.VMEM((cycles * dishes * 2 * rows, wide), F32),
-        ],
-        compiler_params=params(),
-        name="nulls",
-    )(sat_index[:, 0], sat_a[:, 0], sat_b[:, 0], offsets, angles, x)
-    from_b = swap(to_b, 1)
-    from_a = swap(to_a, 0)
+    vectors = jax.ShapeDtypeStruct((dishes, 2 * slots, ports), F32)
+    nulls = []
+    for cycle in range(cycles):
+        own, to_a, to_b = pl.pallas_call(
+            functools.partial(nulls_kernel, cycle),
+            out_shape=(vectors,) * 3,
+            in_specs=[smem(), smem(), smem(), vmem(), vmem(), vmem()],
+            out_specs=(vmem(),) * 3,
+            scratch_shapes=[
+                pltpu.VMEM((rows, ports), F32),
+                pltpu.VMEM((dishes, 4 * rows, samples), F32),
+                pltpu.VMEM((dishes * 2 * rows, wide), F32),
+            ],
+            compiler_params=params(),
+        )(sat_index[:, 0], sat_a[:, 0], sat_b[:, 0], offsets, angles, x)
+        from_b = swap(to_b, 1)
+        from_a = swap(to_a, 0)
+        nulls.append((own, from_a, from_b))
 
     next_rows = jax.ShapeDtypeStruct((dishes, 2 * chans * pad_beams, ports), BF16)
     second_near, second_mine, *second_far, w_next = pl.pallas_call(
@@ -420,18 +418,18 @@
         scratch_shapes=[stage],
         compiler_params=params(),
         name="next_beams",
-    )(x, weights, own, from_a, from_b, first_near, *first_got)
+    )(x, weights, *nulls[0], first_near, *first_got)
     second_got = [step_over(value, k + 2) for k, value in enumerate(second_far)]
     near_got = step_over(second_near, 1)
 
     new_weights = pl.pallas_call(
-        functools.partial(last_nulls_kernel, dims, 1),
+        functools.partial(last_nulls_kernel, dims),
         out_shape=jax.ShapeDtypeStruct(weights.shape, BF16),
         in_specs=[vmem()] * 4,
         out_specs=vmem(),
         compiler_params=params(),
         name="last_nulls",
-    )(w_next, own, from_a, from_b)
+    )(w_next, *nulls[1])
 
     all_dishes = dishes * groups
     pairs = group_beams * chans

time: 33 us -> 36.4 us (1.10)
  the two profiles are of different devices: /device:TPU:17 before, /device:TPU:16 now
where the time goes in v4:
time: 36.4 us; the launch traced here: 36.2 us
  waiting for transfers between devices  12 us (33%)
  Pallas kernels  11.3 us (31%)
  starting transfers between devices  9.37 us (26%)
  local copies, waits for them, and re-layouts  2.85 us (8%)
  between operations  0.73 us (2%)
    ppermute x6, waiting for transfers between devices, swap(): return lax.ppermute(value, ('chan', 'section'), path)  12 us
    ppermute x6, starting transfers between devices, swap(): return lax.ppermute(value, ('chan', 'section'), path)  5.86 us
    pallas_call x2, Pallas kernels, per_device(): pl.pallas_call(functools.partial(nulls_kernel, cycle), out_shape=(vectors...  4.26 us
    ppermute x4, starting transfers between devices, step_over(): lax.ppermute(value, 'section', [(i, i ^ step) for i in range(groups)])  3.5 us
    unnamed x10, local copies, waits for them, and re-layouts  2.85 us
    pallas_call x1, Pallas kernels, per_device(): pl.pallas_call(functools.partial(next_beams_kernel, dims, 0), out_shape=(...  2.48 us
    pallas_call x1, Pallas kernels, per_device(): pl.pallas_call(functools.partial(correlate_kernel, dims, 1.0 / (cycles *...  1.62 us
    pallas_call x1, Pallas kernels, per_device(): pl.pallas_call(functools.partial(last_nulls_kernel, dims), out_shape=jax....  1.5 us
  transfers between devices with their start and end apart: 10, of which 6 were waited for; matrix products, arithmetic and copies ran while one was open for 4% of the time, Pallas kernels for 16%

profile of v4, /device:TPU:16, one launch (start us, length us, event | category | flops | bytes accessed | tf_op | source)
XLA Modules:
  0.0 36.2 jit_solution(3925108146324087957)
XLA Ops:
  0.6 1.3 %copy.7.w_ref = bf16[2,9,2,36,188]{4,3,2,1,0:T(8,128)(2,1)S(1)} copy(bf16[2,9,2,36,188]{4,2,3,1,0:T(2,128)(2,1)} %param.6) | data formatting | bytes 974592 | tf_op args[1]
  2.0 0.6 %spread.1.wide_ref = bf16[9,2,160,376]{3,2,1,0:T(8,128)(2,1)S(1)} custom-call(bf16[2,9,2,36,188]{4,3,2,1,0:T(8,128)(2,1)S(1)} %copy.7.w_ref), custom_call_target="tpu_custom_call" | custom-call | tf_op jit(solution)/shard_map/spread/pallas_call | solution.py:373
  2.6 0.0 copy-start.2
  2.6 0.0 copy-start.1
  2.7 0.0 copy-start.3
  2.7 0.1 copy-done
  2.8 0.8 %first_beams.1 = (bf16[324,128]{1,0:T(8,128)(2,1)S(1)}, bf16[324,128]{1,0:T(8,128)(2,1)S(1)}, bf16[2,324,128]{2,1,0:T(8,128)(2,1)S(1)}) custom-call(bf16[2,2,9,376,128]{4,3,2,1,0:T(8,128)(2,1)S(1)} %bitcast.6, bf16[9,2,160,376]{3,2,1,0:T(8,128)(2,1)S(1)} %spread.1.wide_ref), custom_call_target="tpu_custom_call" | custom-call | tf_op jit(solution)/shard_map/first_beams/pallas_call | solution.py:381
  3.6 1.6 %collective-permute-start.4 = (bf16[2,324,128]{2,1,0:T(8,128)(2,1)S(1)}, bf16[2,324,128]{2,1,0:T(8,128)(2,1)S(1)}, u32[]{:S(2)}, u32[]{:S(2)}) collective-permute-start(bf16[2,324,128]{2,1,0:T(8,128)(2,1)S(1)} %get-tuple-element.21), channel_id=1, source_target_pairs={{0,2},{1,3},{2,0},{3,1},{4,6},{5,7},{6,4},{7,5},{8,10},{9,11},{10,... | collective-permute-start | bytes 497672 | tf_op jit(solution)/shard_map/ppermute | solution.py:362
  5.2 1.5 %collective-permute-start = (s32[2,1,2]{2,1,0:T(1,128)S(1)}, s32[2,1,2]{2,1,0:T(1,128)S(1)}, u32[]{:S(2)}, u32[]{:S(2)}) collective-permute-start(s32[2,1,2]{2,1,0:T(1,128)S(1)} %copy-done.2), channel_id=1, source_target_pairs={{0,4},{1,5},{2,6},{3,7},{4,0},{5,1},{6,2},{7,3},{8,12},{9,13},{10,... | collective-permute-start | bytes 56 | tf_op jit(solution)/shard_map/ppermute | solution.py:356
  6.7 0.4 %collective-permute-start.1 = (s32[2,1,2]{2,1,0:T(1,128)S(1)}, s32[2,1,2]{2,1,0:T(1,128)S(1)}, u32[]{:S(2)}, u32[]{:S(2)}) collective-permute-start(s32[2,1,2]{2,1,0:T(1,128)S(1)} %copy-done.2), channel_id=1, source_target_pairs={{0,1},{1,0},{2,3},{3,2},{4,8},{5,9},{6,10},{7,11},{8,4},{9,5},{10,... | collective-permute-start | bytes 56 | tf_op jit(solution)/shard_map/ppermute | solution.py:356
  7.1 1.7 %collective-permute-done = s32[2,1,2]{2,1,0:T(1,128)S(1)} collective-permute-done((s32[2,1,2]{2,1,0:T(1,128)S(1)}, s32[2,1,2]{2,1,0:T(1,128)S(1)}, u32[]{:S(2)}, u32[]{:S(2)}) %collective-permute-start) | collective-permute-done | bytes 48 | tf_op jit(solution)/shard_map/ppermute | solution.py:356
  8.8 2.4 %collective-permute-done.1 = s32[2,1,2]{2,1,0:T(1,128)S(1)} collective-permute-done((s32[2,1,2]{2,1,0:T(1,128)S(1)}, s32[2,1,2]{2,1,0:T(1,128)S(1)}, u32[]{:S(2)}, u32[]{:S(2)}) %collective-permute-start.1) | collective-permute-done | bytes 48 | tf_op jit(solution)/shard_map/ppermute | solution.py:356
  11.2 2.1 %shard_map.68 = (f32[9,4,188]{2,1,0:T(4,128)S(1)}, f32[9,4,188]{2,1,0:T(4,128)S(1)}, f32[9,4,188]{2,1,0:T(4,128)S(1)}) custom-call(s32[2,2]{1,0:T(2,128)S(1)} %bitcast.10, s32[2,2]{1,0:T(2,128)S(1)} %bitcast.12, s32[2,2]{1,0:T(2,128)S(1)} %bitcast.14, s32[2,128]{1,0:T(2,128)S(1)} %copy-done.3, f32[64,188]{1,0:T(8,128)S(1)} %copy-done.1, ...), custom_call_target="tpu_custom_call" | custom-call | tf_op jit(solution)/shard_map/pallas_call | solution.py:396
  13.3 0.6 %collective-permute-start.2 = (f32[9,4,188]{2,1,0:T(4,128)S(1)}, f32[9,4,188]{2,1,0:T(4,128)S(1)}, u32[]{:S(2)}, u32[]{:S(2)}) collective-permute-start(f32[9,4,188]{2,1,0:T(4,128)S(1)} %get-tuple-element.18), channel_id=1, source_target_pairs={{0,4},{1,5},{2,6},{3,7},{4,0},{5,1},{6,2},{7,3},{8,12},{9,13},{10,... | collective-permute-start | bytes 81224 | tf_op jit(solution)/shard_map/ppermute | solution.py:356
  13.9 1.4 %collective-permute-start.3 = (f32[9,4,188]{2,1,0:T(4,128)S(1)}, f32[9,4,188]{2,1,0:T(4,128)S(1)}, u32[]{:S(2)}, u32[]{:S(2)}) collective-permute-start(f32[9,4,188]{2,1,0:T(4,128)S(1)} %get-tuple-element.19), channel_id=1, source_target_pairs={{0,1},{1,0},{2,3},{3,2},{4,8},{5,9},{6,10},{7,11},{8,4},{9,5},{10,... | collective-permute-start | bytes 81224 | tf_op jit(solution)/shard_map/ppermute | solution.py:356
  15.3 2.0 %collective-permute-done.2.a_ref = f32[9,4,188]{2,1,0:T(4,128)S(1)} collective-permute-done((f32[9,4,188]{2,1,0:T(4,128)S(1)}, f32[9,4,188]{2,1,0:T(4,128)S(1)}, u32[]{:S(2)}, u32[]{:S(2)}) %collective-permute-start.2) | collective-permute-done | bytes 27104 | tf_op jit(solution)/shard_map/ppermute | solution.py:356
  17.3 1.4 %collective-permute-done.3.b_ref = f32[9,4,188]{2,1,0:T(4,128)S(1)} collective-permute-done((f32[9,4,188]{2,1,0:T(4,128)S(1)}, f32[9,4,188]{2,1,0:T(4,128)S(1)}, u32[]{:S(2)}, u32[]{:S(2)}) %collective-permute-start.3) | collective-permute-done | bytes 27104 | tf_op jit(solution)/shard_map/ppermute | solution.py:356
  18.8 0.0 collective-permute-done.4.refs_0_.refs_3_
  18.8 2.5 %next_beams.1 = (bf16[3,324,128]{2,1,0:T(8,128)(2,1)S(1)}, bf16[324,128]{1,0:T(8,128)(2,1)S(1)}, bf16[324,128]{1,0:T(8,128)(2,1)S(1)}, bf16[324,128]{1,0:T(8,128)(2,1)S(1)}, bf16[9,160,188]{2,1,0:T(8,128)(2,1)S(1)}) custom-call(bf16[2,2,9,376,128]{4,3,2,1,0:T(8,128)(2,1)S(1)} %bitcast.8, bf16[2,9,2,36,188]{4,3,2,1,0:T(8,128)(2,1)S(1)} %copy.7.w_ref, ...), custom_call_target="tpu_custom_call" | custom-call | tf_op jit(solution)/shard_map/next_beams/pallas_call | solution.py:413
  21.3 0.1 collective-permute-start.5
  21.3 0.6 %collective-permute-start.6 = (bf16[324,128]{1,0:T(8,128)(2,1)S(1)}, bf16[324,128]{1,0:T(8,128)(2,1)S(1)}, u32[]{:S(2)}, u32[]{:S(2)}) collective-permute-start(bf16[324,128]{1,0:T(8,128)(2,1)S(1)} %get-tuple-element.24), channel_id=1, source_target_pairs={{0,2},{1,3},{2,0},{3,1},{4,6},{5,7},{6,4},{7,5},{8,10},{9,11},{10,... | collective-permute-start | bytes 248840 | tf_op jit(solution)/shard_map/ppermute | solution.py:362
  21.9 1.3 %collective-permute-start.7 = (bf16[324,128]{1,0:T(8,128)(2,1)S(1)}, bf16[324,128]{1,0:T(8,128)(2,1)S(1)}, u32[]{:S(2)}, u32[]{:S(2)}) collective-permute-start(bf16[324,128]{1,0:T(8,128)(2,1)S(1)} %get-tuple-element.25), channel_id=1, source_target_pairs={{0,3},{1,2},{2,1},{3,0},{4,7},{5,6},{6,5},{7,4},{8,11},{9,10},{10,... | collective-permute-start | bytes 248840 | tf_op jit(solution)/shard_map/ppermute | solution.py:362
  23.2 2.1 %shard_map.69 = (f32[9,4,188]{2,1,0:T(4,128)S(1)}, f32[9,4,188]{2,1,0:T(4,128)S(1)}, f32[9,4,188]{2,1,0:T(4,128)S(1)}) custom-call(s32[2,2]{1,0:T(2,128)S(1)} %bitcast.11, s32[2,2]{1,0:T(2,128)S(1)} %bitcast.13, s32[2,2]{1,0:T(2,128)S(1)} %bitcast.15, s32[2,128]{1,0:T(2,128)S(1)} %copy-done.3, f32[64,188]{1,0:T(8,128)S(1)} %copy-done.1, ...), custom_call_target="tpu_custom_call" | custom-call | tf_op jit(solution)/shard_map/pallas_call | solution.py:396
  25.3 1.6 %collective-permute-start.8 = (f32[9,4,188]{2,1,0:T(4,128)S(1)}, f32[9,4,188]{2,1,0:T(4,128)S(1)}, u32[]{:S(2)}, u32[]{:S(2)}) collective-permute-start(f32[9,4,188]{2,1,0:T(4,128)S(1)} %get-tuple-element.28), channel_id=1, source_target_pairs={{0,4},{1,5},{2,6},{3,7},{4,0},{5,1},{6,2},{7,3},{8,12},{9,13},{10,... | collective-permute-start | bytes 81224 | tf_op jit(solution)/shard_map/ppermute | solution.py:356
  26.9 0.4 %collective-permute-start.9 = (f32[9,4,188]{2,1,0:T(4,128)S(1)}, f32[9,4,188]{2,1,0:T(4,128)S(1)}, u32[]{:S(2)}, u32[]{:S(2)}) collective-permute-start(f32[9,4,188]{2,1,0:T(4,128)S(1)} %get-tuple-element.29), channel_id=1, source_target_pairs={{0,1},{1,0},{2,3},{3,2},{4,8},{5,9},{6,10},{7,11},{8,4},{9,5},{10,... | collective-permute-start | bytes 81224 | tf_op jit(solution)/shard_map/ppermute | solution.py:356
  27.3 2.0 %collective-permute-done.8.a_ref = f32[9,4,188]{2,1,0:T(4,128)S(1)} collective-permute-done((f32[9,4,188]{2,1,0:T(4,128)S(1)}, f32[9,4,188]{2,1,0:T(4,128)S(1)}, u32[]{:S(2)}, u32[]{:S(2)}) %collective-permute-start.8) | collective-permute-done | bytes 27104 | tf_op jit(solution)/shard_map/ppermute | solution.py:356
  29.3 2.4 %collective-permute-done.9.b_ref = f32[9,4,188]{2,1,0:T(4,128)S(1)} collective-permute-done((f32[9,4,188]{2,1,0:T(4,128)S(1)}, f32[9,4,188]{2,1,0:T(4,128)S(1)}, u32[]{:S(2)}, u32[]{:S(2)}) %collective-permute-start.9) | collective-permute-done | bytes 27104 | tf_op jit(solution)/shard_map/ppermute | solution.py:356
  31.7 1.5 %last_nulls.1 = bf16[2,9,2,36,188]{4,3,2,1,0:T(8,128)(2,1)S(1)} custom-call(bf16[9,160,188]{2,1,0:T(8,128)(2,1)S(1)} %get-tuple-element.26.w_ref, f32[9,4,188]{2,1,0:T(4,128)S(1)} %get-tuple-element.27.own_ref, f32[9,4,188]{2,1,0:T(4,128)S(1)} %collective-permute-done.8.a_ref, f32[9,4,188]{2,1,0:T(4,128)S(1)} %collective-permute-done.9.b_ref), custom_call_target="tpu_custom_call" | custom-call | tf_op jit(solution)/shard_map/last_nulls/pallas_call | solution.py:425
  33.2 1.4 %copy.9 = bf16[2,9,2,36,188]{4,2,3,1,0:T(2,128)(2,1)} copy(bf16[2,9,2,36,188]{4,3,2,1,0:T(8,128)(2,1)S(1)} %last_nulls.1) | data formatting | bytes 974592
  34.6 0.0 collective-permute-done.6.refs_4_
  34.6 0.0 collective-permute-done.7.refs_5_
  34.6 1.6 %correlate.1 = f32[2,9,2,1296]{3,2,1,0:T(2,128)} custom-call(bf16[324,128]{1,0:T(8,128)(2,1)S(1)} %get-tuple-element.16.refs_0_, bf16[324,128]{1,0:T(8,128)(2,1)S(1)} %get-tuple-element.22.refs_1_, bf16[3,324,128]{2,1,0:T(8,128)(2,1)S(1)} %collective-permute-done.5.refs_2_, bf16[2,324,128]{2,1,0:T(8,128)(2,1)S(1)} %collective-permute-done.4.refs_0_.refs_3_, ...), custom_call_target="tpu_custom_call" | custom-call | tf_op jit(solution)/shard_map/correlate/pallas_call | solution.py:437
  (5 shorter events, 0.0 us)
Async XLA Ops:
  0.6 2.2 %copy-start = (bf16[2,2,9,2,188,128]{5,3,4,2,1,0:T(2,128)(2,1)S(1)}, bf16[2,2,9,2,188,128]{5,3,4,2,1,0:T(2,128)(2,1)}, u32[]{:S(2)}) copy-start(bf16[2,2,9,2,188,128]{5,3,4,2,1,0:T(2,128)(2,1)} %param.5) | copy-start | bytes 10395652
  2.6 2.6 %copy-start.2 = (s32[2,1,2]{2,1,0:T(1,128)S(1)}, s32[2,1,2]{2,1,0:T(1,128)}, u32[]{:S(2)}) copy-start(s32[2,1,2]{2,1,0:T(1,128)} %param.7) | copy-start | bytes 52
  2.6 8.5 %copy-start.1 = (f32[64,188]{1,0:T(8,128)S(1)}, f32[64,188]{1,0:T(8,128)}, u32[]{:S(2)}) copy-start(f32[64,188]{1,0:T(8,128)} %ang_ref.3) | copy-start | bytes 144388
  2.7 8.5 %copy-start.3 = (s32[2,128]{1,0:T(2,128)S(1)}, s32[2,128]{1,0:T(2,128)}, u32[]{:S(2)}) copy-start(s32[2,128]{1,0:T(2,128)} %off_ref.3) | copy-start | bytes 3076
  3.6 15.2 %collective-permute-start.4 = (bf16[2,324,128]{2,1,0:T(8,128)(2,1)S(1)}, bf16[2,324,128]{2,1,0:T(8,128)(2,1)S(1)}, u32[]{:S(2)}, u32[]{:S(2)}) collective-permute-start(bf16[2,324,128]{2,1,0:T(8,128)(2,1)S(1)} %get-tuple-element.21), channel_id=1, source_target_pairs={{0,2},{1,3},{2,0},{3,1},{4,6},{5,7},{6,4},{7,5},{8,10},{9,11},{10,... | collective-permute-start | bytes 497672 | tf_op jit(solution)/shard_map/ppermute | solution.py:362
  5.2 3.6 %collective-permute-start = (s32[2,1,2]{2,1,0:T(1,128)S(1)}, s32[2,1,2]{2,1,0:T(1,128)S(1)}, u32[]{:S(2)}, u32[]{:S(2)}) collective-permute-start(s32[2,1,2]{2,1,0:T(1,128)S(1)} %copy-done.2), channel_id=1, source_target_pairs={{0,4},{1,5},{2,6},{3,7},{4,0},{5,1},{6,2},{7,3},{8,12},{9,13},{10,... | collective-permute-start | bytes 56 | tf_op jit(solution)/shard_map/ppermute | solution.py:356
  6.7 4.5 %collective-permute-start.1 = (s32[2,1,2]{2,1,0:T(1,128)S(1)}, s32[2,1,2]{2,1,0:T(1,128)S(1)}, u32[]{:S(2)}, u32[]{:S(2)}) collective-permute-start(s32[2,1,2]{2,1,0:T(1,128)S(1)} %copy-done.2), channel_id=1, source_target_pairs={{0,1},{1,0},{2,3},{3,2},{4,8},{5,9},{6,10},{7,11},{8,4},{9,5},{10,... | collective-permute-start | bytes 56 | tf_op jit(solution)/shard_map/ppermute | solution.py:356
  13.3 4.0 %collective-permute-start.2 = (f32[9,4,188]{2,1,0:T(4,128)S(1)}, f32[9,4,188]{2,1,0:T(4,128)S(1)}, u32[]{:S(2)}, u32[]{:S(2)}) collective-permute-start(f32[9,4,188]{2,1,0:T(4,128)S(1)} %get-tuple-element.18), channel_id=1, source_target_pairs={{0,4},{1,5},{2,6},{3,7},{4,0},{5,1},{6,2},{7,3},{8,12},{9,13},{10,... | collective-permute-start | bytes 81224 | tf_op jit(solution)/shard_map/ppermute | solution.py:356
  13.9 4.9 %collective-permute-start.3 = (f32[9,4,188]{2,1,0:T(4,128)S(1)}, f32[9,4,188]{2,1,0:T(4,128)S(1)}, u32[]{:S(2)}, u32[]{:S(2)}) collective-permute-start(f32[9,4,188]{2,1,0:T(4,128)S(1)} %get-tuple-element.19), channel_id=1, source_target_pairs={{0,1},{1,0},{2,3},{3,2},{4,8},{5,9},{6,10},{7,11},{8,4},{9,5},{10,... | collective-permute-start | bytes 81224 | tf_op jit(solution)/shard_map/ppermute | solution.py:356
  21.3 13.3 %collective-permute-start.5 = (bf16[3,324,128]{2,1,0:T(8,128)(2,1)S(1)}, bf16[3,324,128]{2,1,0:T(8,128)(2,1)S(1)}, u32[]{:S(2)}, u32[]{:S(2)}) collective-permute-start(bf16[3,324,128]{2,1,0:T(8,128)(2,1)S(1)} %get-tuple-element.23), channel_id=1, source_target_pairs={{0,1},{1,0},{2,3},{3,2},{4,5},{5,4},{6,7},{7,6},{8,9},{9,8},{10,11... | collective-permute-start | bytes 746504 | tf_op jit(solution)/shard_map/ppermute | solution.py:362
  21.3 13.2 %collective-permute-start.6 = (bf16[324,128]{1,0:T(8,128)(2,1)S(1)}, bf16[324,128]{1,0:T(8,128)(2,1)S(1)}, u32[]{:S(2)}, u32[]{:S(2)}) collective-permute-start(bf16[324,128]{1,0:T(8,128)(2,1)S(1)} %get-tuple-element.24), channel_id=1, source_target_pairs={{0,2},{1,3},{2,0},{3,1},{4,6},{5,7},{6,4},{7,5},{8,10},{9,11},{10,... | collective-permute-start | bytes 248840 | tf_op jit(solution)/shard_map/ppermute | solution.py:362
  21.9 12.7 %collective-permute-start.7 = (bf16[324,128]{1,0:T(8,128)(2,1)S(1)}, bf16[324,128]{1,0:T(8,128)(2,1)S(1)}, u32[]{:S(2)}, u32[]{:S(2)}) collective-permute-start(bf16[324,128]{1,0:T(8,128)(2,1)S(1)} %get-tuple-element.25), channel_id=1, source_target_pairs={{0,3},{1,2},{2,1},{3,0},{4,7},{5,6},{6,5},{7,4},{8,11},{9,10},{10,... | collective-permute-start | bytes 248840 | tf_op jit(solution)/shard_map/ppermute | solution.py:362
  25.3 4.0 %collective-permute-start.8 = (f32[9,4,188]{2,1,0:T(4,128)S(1)}, f32[9,4,188]{2,1,0:T(4,128)S(1)}, u32[]{:S(2)}, u32[]{:S(2)}) collective-permute-start(f32[9,4,188]{2,1,0:T(4,128)S(1)} %get-tuple-element.28), channel_id=1, source_target_pairs={{0,4},{1,5},{2,6},{3,7},{4,0},{5,1},{6,2},{7,3},{8,12},{9,13},{10,... | collective-permute-start | bytes 81224 | tf_op jit(solution)/shard_map/ppermute | solution.py:356
  26.9 4.9 %collective-permute-start.9 = (f32[9,4,188]{2,1,0:T(4,128)S(1)}, f32[9,4,188]{2,1,0:T(4,128)S(1)}, u32[]{:S(2)}, u32[]{:S(2)}) collective-permute-start(f32[9,4,188]{2,1,0:T(4,128)S(1)} %get-tuple-element.29), channel_id=1, source_target_pairs={{0,1},{1,0},{2,3},{3,2},{4,8},{5,9},{6,10},{7,11},{8,4},{9,5},{10,... | collective-permute-start | bytes 81224 | tf_op jit(solution)/shard_map/ppermute | solution.py:356
